TPU v7x, 32 devices: a whole 2x2x4 slice. The times are simulated.
32 devices in a mesh: reach: 2 (over y), row: 4 (over z), col: 4 (over x, core).
Axes of the slice: x: 2, y: 2, z: 4, core: 2. Of those that a mesh axis runs over, the one named last changes fastest.
Arguments:
- operator: float32 [2048, 65536], P(('reach', 'col'), 'row'), parts along dimension 0, may hold values from -0.03125 to 0.03125
- basis: float32 [131072, 256], P(('reach', 'row')), parts along dimension 0, may hold values from -6 to 6
Outputs:
- image: float32 [2048, 256], P(('reach', 'row')), parts along dimension 0
There are 2 independent parts, one for each index of `reach`. A program takes and returns all parts, laid end to end along the dimension named above; each array names one. Nothing has to cross between parts.
All inputs are finite; a program needn't handle non-finite values.
Results may differ from a plain program's by a relative error of at most 0.000071.
Values sent between devices are 32-bit elements; how exact they have to be, the bound alone decides.
No kernel may reach another device: no remote copies, remote signals or barrier semaphores. Data moves between devices by JAX's collectives and lax.ppermute only.
A program may use at most 64 MiB of HBM per device.

v0:
```python
import jax
import jax.numpy as jnp
from jax import lax
from jax.sharding import PartitionSpec as P


def spread(value, axis, source):
    kept = jnp.where(lax.axis_index(axis) == source, value, 0).astype(value.dtype)
    return lax.psum(kept, axis)


def shards(operator, basis):
    partial_sum = jnp.dot(
        operator, basis, preferred_element_type=jnp.float32, precision=lax.Precision.HIGHEST
    )
    tile_rows = operator.shape[0]
    n_row = lax.axis_size("row")
    n_col = lax.axis_size("col")
    group = n_row // n_col
    out_rows = tile_rows * n_col // n_row
    summed = lax.psum(partial_sum, "row")
    row_index = lax.axis_index("row")
    offset = row_index % group * out_rows
    picked = lax.dynamic_slice_in_dim(summed, offset, out_rows, 0)
    return spread(picked, "col", row_index // group)


def solution(mesh):
    in_specs = (P(("reach", "col"), "row"), P(("reach", "row"), None))
    out_specs = P(("reach", "row"), None)
    return jax.shard_map(shards, mesh=mesh, in_specs=in_specs, out_specs=out_specs, check_vma=False)
```

profile of v0, /device:TPU:0, one launch (start us, length us, event | category | flops | bytes accessed | tf_op | source)
XLA Modules:
  0.0 106.0 jit_solution(11191584294463896214)
XLA Ops:
  6.5 0.0 all-reduce.3.cloned.1.call-start
  6.5 18.6 %fusion = f32[256,256]{1,0:T(8,128)} fusion(f32[256,16384]{1,0:T(8,128)} %param.2, f32[16384,256]{1,0:T(8,128)} %param.3), kind=kOutput, calls=%fused_computation.1 | convolution fusion | flops 12884901888 | bytes 33816576 | tf_op jit(solution)/shard_map/dot_general | solution.py:13
  25.2 0.0 all-reduce.3.cloned.1.call-update
  25.2 0.0 all-reduce.5.cloned.1.call-start
  25.2 38.1 %all-reduce.3.cloned.1.call-done = f32[256,256]{1,0:T(8,128)} async-done(((f32[256,256]{1,0:T(8,128)}), f32[256,256]{1,0:T(8,128)}) %all-reduce.3.cloned.1.call-update) | async-done | bytes 262160 | tf_op jit(solution)/shard_map/psum | solution.py:21
  63.3 1.7 %broadcast_select_fusion = f32[256,256]{1,0:T(8,128)} fusion(f32[256,256]{1,0:T(8,128)} %all-reduce.3.cloned.1.call-done, pred[]{:T(512)S(6)} %eq.5), kind=kLoop, calls=%fused_computation | loop fusion | flops 65536 | bytes 524289 | tf_op jit(solution)/shard_map/jit(_where)/select_n | solution.py:8
  65.0 0.0 all-reduce.5.cloned.1.call-update
  65.0 32.5 %all-reduce.5.cloned.1.call-done = f32[256,256]{1,0:T(8,128)} async-done(((f32[256,256]{1,0:T(8,128)}), f32[256,256]{1,0:T(8,128)}) %all-reduce.5.cloned.1.call-update) | async-done | bytes 262160 | tf_op jit(solution)/shard_map/psum | solution.py:9
  97.5 1.7 %copy.5 = f32[256,256]{1,0:T(8,128)} copy(f32[256,256]{1,0:T(8,128)} %all-reduce.5.cloned.1.call-done) | data formatting | bytes 524288
Async XLA Ops:
  6.5 56.8 %all-reduce.3.cloned.1.call-start = ((), (), s32[]{:S(2)}) async-start(), calls=%async_computation | async-start | bytes 524288 | tf_op jit(solution)/shard_map/psum | solution.py:21
  25.2 72.3 %all-reduce.5.cloned.1.call-start = ((), (), s32[]{:S(2)}) async-start(), calls=%async_computation.1 | async-start | bytes 524288 | tf_op jit(solution)/shard_map/psum | solution.py:9
Sparse Core Ops, SparseCore 0:
  25.3 37.9 all-reduce.2
  65.8 31.6 all-reduce.4
where the time goes:
time: 106 us
  waiting for transfers between devices  70.6 us (67%)
  matrix products  18.6 us (18%)
  between operations  13.4 us (13%)
  other arithmetic  1.67 us (2%)
  local copies, waits for them, and re-layouts  1.67 us (2%)
    psum x1, waiting for transfers between devices, shards(): summed = lax.psum(partial_sum, 'row')  38.1 us
    psum x1, waiting for transfers between devices, spread(): return lax.psum(kept, axis)  32.5 us
    dot_general x1, matrix products, shards(): jnp.dot(operator, basis, preferred_element_type=jnp.float32, precision=la...  18.6 us
  transfers between devices with their start and end apart: 2, of which 2 were waited for; matrix products, arithmetic and copies ran while one was open for 0% of the time, Pallas kernels for 0%

commit v1 on v0

v1 whole, which is shorter than its diff:
```python
import functools

import jax
import jax.numpy as jnp
from jax import lax
from jax.experimental import pallas as pl
from jax.experimental.pallas import tpu as pltpu
from jax.sharding import PartitionSpec as P

CHUNK = 1024
DEPTH = 6


def split(value):
    high = value.astype(jnp.bfloat16)
    low = (value - high.astype(jnp.float32)).astype(jnp.bfloat16)
    return high, low


def dot(a, b):
    return jnp.dot(a, b, preferred_element_type=jnp.float32)


def matmul_kernel(steps, chunk, a_hbm, b_hbm, out, a_buf, b_buf, sems):
    def copies(step):
        where = pl.ds(step * chunk, chunk)
        return (
            pltpu.make_async_copy(a_hbm.at[:, where], a_buf.at[step], sems.at[0, step]),
            pltpu.make_async_copy(b_hbm.at[where, :], b_buf.at[step], sems.at[1, step]),
        )

    def start(step):
        for copy in copies(step):
            copy.start()

    for step in range(min(DEPTH, steps)):
        start(step)
    rows = out.shape[0]
    half = rows // 2 if rows % 16 == 0 else rows
    total = jnp.zeros(out.shape, jnp.float32)
    for step in range(steps):
        for copy in copies(step):
            copy.wait()
        if step + DEPTH < steps:
            start(step + DEPTH)
        b_high, b_low = split(b_buf[step])
        parts = []
        for first in range(0, rows, half):
            a_high, a_low = split(a_buf[step, first : first + half])
            parts.append(dot(a_high, b_high) + dot(a_high, b_low) + dot(a_low, b_high))
        total += jnp.concatenate(parts, 0)
    out[...] = total


def matmul(a, b):
    rows, depth = a.shape
    columns = b.shape[1]
    chunk = min(CHUNK, depth)
    steps = depth // chunk
    return pl.pallas_call(
        functools.partial(matmul_kernel, steps, chunk),
        out_shape=jax.ShapeDtypeStruct((rows, columns), jnp.float32),
        in_specs=[pl.BlockSpec(memory_space=pl.ANY)] * 2,
        out_specs=pl.BlockSpec(memory_space=pltpu.VMEM),
        scratch_shapes=[
            pltpu.VMEM((steps, rows, chunk), jnp.float32),
            pltpu.VMEM((steps, chunk, columns), jnp.float32),
            pltpu.SemaphoreType.DMA((2, steps)),
        ],
        compiler_params=pltpu.CompilerParams(vmem_limit_bytes=60 * 2**20),
    )(a, b)


def permute(value, n_row, n_col, target):
    pairs = []
    for r in range(n_row):
        for c in range(n_col):
            to_r, to_c = target(r, c)
            pairs.append((r * n_col + c, to_r * n_col + to_c))
    return lax.ppermute(value, ("row", "col"), pairs)


def general(partial, n_row, n_col):
    rows = partial.shape[0]
    group = n_row // n_col
    out_rows = rows // group
    summed = lax.psum(partial, "row")
    row = lax.axis_index("row")
    picked = lax.dynamic_slice_in_dim(summed, row % group * out_rows, out_rows, 0)
    kept = jnp.where(lax.axis_index("col") == row // group, picked, 0)
    return lax.psum(kept, "col")


def square(partial, n_row, n_col):
    row, col = lax.axis_index("row"), lax.axis_index("col")
    half = partial.shape[0] // 2
    side = row // 2
    near = lax.dynamic_slice_in_dim(partial, side * half, half, 0)
    far = lax.dynamic_slice_in_dim(partial, (1 - side) * half, half, 0)
    near = permute(near, n_row, n_col, lambda r, c: (c, (r // 2) * 2 + r % 2))
    far = permute(far, n_row, n_col, lambda r, c: (c, (1 - r // 2) * 2 + r % 2))
    mine = near + far
    mine = mine + lax.ppermute(mine, "col", [(c, c ^ 1) for c in range(n_col)])
    other = lax.ppermute(mine, "col", [(c, c ^ 2) for c in range(n_col)])
    first = col < 2
    return jnp.concatenate([jnp.where(first, mine, other), jnp.where(first, other, mine)], 0)


def shards(operator, basis):
    partial = matmul(operator, basis)
    n_row, n_col = lax.axis_size("row"), lax.axis_size("col")
    if n_row == 4 and n_col == 4 and partial.shape[0] % 16 == 0:
        return square(partial, n_row, n_col)
    return general(partial, n_row, n_col)


def solution(mesh):
    in_specs = (P(("reach", "col"), "row"), P(("reach", "row"), None))
    out_specs = P(("reach", "row"), None)
    return jax.shard_map(shards, mesh=mesh, in_specs=in_specs, out_specs=out_specs, check_vma=False)
```

time: 106 us -> 37.8 us (0.36)
  waiting for transfers between devices: 70.6 us -> 14.1 us
  matrix products: 18.6 us -> 0 us
  between operations: 13.4 us -> 0.04 us
  Pallas kernels: 0 us -> 12.4 us
  starting transfers between devices: 0.04 us -> 9.33 us
    psum x2 -> x0, waiting for transfers between devices: 70.6 us -> none  [the longest x1 38.1 us: shards(): summed = lax.psum(partial_sum, 'row')]
    dot_general x1 -> x0, matrix products: 18.6 us -> none  [shards(): jnp.dot(operator, basis, preferred_element_type=jnp.float32, precision=la...]
    ppermute x0 -> x4, waiting for transfers between devices: none -> 14.1 us  [the longest x2 9 us: permute(): return lax.ppermute(value, ('row', 'col'), pairs)]
    pallas_call x0 -> x1, Pallas kernels: none -> 12.4 us  [matmul(): pl.pallas_call(functools.partial(matmul_kernel, steps, chunk), out_shape=...]
    ppermute x0 -> x4, starting transfers between devices: none -> 9.33 us  [the longest x1 5.61 us: square(): other = lax.ppermute(mine, 'col', [(c, c ^ 2) for c in range(n_col)])]
    unnamed x1 -> x0, local copies, waits for them, and re-layouts: 1.67 us -> none
    select_n x1, other arithmetic: 1.67 us -> 0.02 us  [square(): jnp.where(first, mine, other)]
  transfers between devices with their start and end apart: 2 -> 4, of which waited for: 2 -> 3; matrix products, arithmetic and copies ran while one was open for 0% -> 0% of each run, Pallas kernels for 0% -> 0%
where the time goes in v1:
time: 37.8 us; the launch traced here: 37.7 us
  waiting for transfers between devices  14.1 us (37%)
  Pallas kernels  12.4 us (33%)
  starting transfers between devices  9.33 us (25%)
  local copies, waits for them, and re-layouts  0.99 us (3%)
  other arithmetic  0.77 us (2%)
    pallas_call x1, Pallas kernels, matmul(): pl.pallas_call(functools.partial(matmul_kernel, steps, chunk), out_shape=...  12.4 us
    ppermute x2, waiting for transfers between devices, permute(): return lax.ppermute(value, ('row', 'col'), pairs)  9 us
    ppermute x1, starting transfers between devices, square(): other = lax.ppermute(mine, 'col', [(c, c ^ 2) for c in range(n_col)])  5.61 us
    ppermute x1, waiting for transfers between devices, square(): other = lax.ppermute(mine, 'col', [(c, c ^ 2) for c in range(n_col)])  3.81 us
    ppermute x2, starting transfers between devices, permute(): return lax.ppermute(value, ('row', 'col'), pairs)  3.65 us
    ppermute x1, waiting for transfers between devices, square(): mine = mine + lax.ppermute(mine, 'col', [(c, c ^ 1) for c in range(n_col)])  1.33 us
    dynamic_slice x1, local copies, waits for them, and re-layouts, square(): far = lax.dynamic_slice_in_dim(partial, (1 - side) * half, half, 0)  0.99 us
  transfers between devices with their start and end apart: 4, of which 3 were waited for; matrix products, arithmetic and copies ran while one was open for 0% of the time, Pallas kernels for 0%

profile of v1, /device:TPU:0, one launch (start us, length us, event | category | flops | bytes accessed | tf_op | source)
XLA Modules:
  0.0 37.7 jit_solution(1119585256688058869)
XLA Ops:
  0.0 12.4 %shard_map.28 = f32[256,256]{1,0:T(8,128)} custom-call(f32[256,16384]{1,0:T(8,128)} %a_hbm.1, f32[16384,256]{1,0:T(8,128)} %b_hbm.1), custom_call_target="tpu_custom_call" | custom-call | tf_op jit(solution)/shard_map/pallas_call | solution.py:60
  12.4 1.0 %constant_dynamic-slice_fusion = (f32[128,256]{1,0:T(8,128)S(1)}, f32[128,256]{1,0:T(8,128)S(1)}) fusion(f32[256,256]{1,0:T(8,128)} %shard_map.28, s32[]{:T(128)S(6)} %select_n.26, s32[]{:T(128)S(6)} %select_n.25), kind=kLoop, calls=%fused_computation.3 | loop fusion | bytes 524296 | tf_op jit(solution)/shard_map/dynamic_slice | solution.py:99
  13.4 3.0 %collective-permute-start.1 = (f32[128,256]{1,0:T(8,128)S(1)}, f32[128,256]{1,0:T(8,128)S(1)}, u32[]{:S(2)}, u32[]{:S(2)}) collective-permute-start(f32[128,256]{1,0:T(8,128)S(1)} %get-tuple-element.7), channel_id=1, source_target_pairs={{0,2},{1,6},{2,10},{3,14},{4,3},{5,7},{6,11},{7,15},{8,0},{9,4},{1... | collective-permute-start | bytes 393224 | tf_op jit(solution)/shard_map/ppermute | solution.py:80
  16.4 0.7 %collective-permute-start = (f32[128,256]{1,0:T(8,128)S(1)}, f32[128,256]{1,0:T(8,128)S(1)}, u32[]{:S(2)}, u32[]{:S(2)}) collective-permute-start(f32[128,256]{1,0:T(8,128)S(1)} %get-tuple-element.8), channel_id=1, source_target_pairs={{0,0},{1,4},{2,8},{3,12},{4,1},{5,5},{6,9},{7,13},{8,2},{9,6},{10,... | collective-permute-start | bytes 393224 | tf_op jit(solution)/shard_map/ppermute | solution.py:80
  17.0 9.0 %collective-permute-done.1 = f32[128,256]{1,0:T(8,128)S(1)} collective-permute-done((f32[128,256]{1,0:T(8,128)S(1)}, f32[128,256]{1,0:T(8,128)S(1)}, u32[]{:S(2)}, u32[]{:S(2)}) %collective-permute-start.1) | collective-permute-done | bytes 131104 | tf_op jit(solution)/shard_map/ppermute | solution.py:80
  26.0 0.0 collective-permute-done
  26.1 0.1 collective-permute-start.2
  26.1 1.3 %collective-permute-done.2 = f32[128,256]{1,0:T(8,128)S(1)} collective-permute-done((f32[128,256]{1,0:T(8,128)S(1)}, f32[128,256]{1,0:T(8,128)S(1)}, u32[]{:S(2)}, u32[]{:S(2)}) %collective-permute-start.2) | collective-permute-done | bytes 131104 | tf_op jit(solution)/shard_map/ppermute | solution.py:103
  27.5 5.6 %collective-permute-start.3 = (f32[128,256]{1,0:T(8,128)S(1)}, f32[128,256]{1,0:T(8,128)S(1)}, u32[]{:S(2)}, u32[]{:S(2)}) collective-permute-start(f32[128,256]{1,0:T(8,128)S(1)} %add.16), channel_id=1, source_target_pairs={{0,2},{1,3},{2,0},{3,1},{4,6},{5,7},{6,4},{7,5},{8,10},{9,11},{10,... | collective-permute-start | bytes 393224 | tf_op jit(solution)/shard_map/ppermute | solution.py:104
  33.1 3.8 %collective-permute-done.3 = f32[128,256]{1,0:T(8,128)S(1)} collective-permute-done((f32[128,256]{1,0:T(8,128)S(1)}, f32[128,256]{1,0:T(8,128)S(1)}, u32[]{:S(2)}, u32[]{:S(2)}) %collective-permute-start.3) | collective-permute-done | bytes 131104 | tf_op jit(solution)/shard_map/ppermute | solution.py:104
  36.9 0.7 %pad_maximum_fusion = f32[256,256]{1,0:T(8,128)} fusion(f32[128,256]{1,0:T(8,128)S(1)} %get-tuple-element.6, f32[128,256]{1,0:T(8,128)S(1)} %get-tuple-element.5), kind=kLoop, calls=%fused_computation | loop fusion | flops 65536 | bytes 524288 | tf_op jit(solution)/shard_map/concatenate | solution.py:106
  (3 shorter events, 0.1 us)
Async XLA Ops:
  13.4 12.7 %collective-permute-start.1 = (f32[128,256]{1,0:T(8,128)S(1)}, f32[128,256]{1,0:T(8,128)S(1)}, u32[]{:S(2)}, u32[]{:S(2)}) collective-permute-start(f32[128,256]{1,0:T(8,128)S(1)} %get-tuple-element.7), channel_id=1, source_target_pairs={{0,2},{1,6},{2,10},{3,14},{4,3},{5,7},{6,11},{7,15},{8,0},{9,4},{1... | collective-permute-start | bytes 393224 | tf_op jit(solution)/shard_map/ppermute | solution.py:80
  16.4 9.7 %collective-permute-start = (f32[128,256]{1,0:T(8,128)S(1)}, f32[128,256]{1,0:T(8,128)S(1)}, u32[]{:S(2)}, u32[]{:S(2)}) collective-permute-start(f32[128,256]{1,0:T(8,128)S(1)} %get-tuple-element.8), channel_id=1, source_target_pairs={{0,0},{1,4},{2,8},{3,12},{4,1},{5,5},{6,9},{7,13},{8,2},{9,6},{10,... | collective-permute-start | bytes 393224 | tf_op jit(solution)/shard_map/ppermute | solution.py:80
  26.1 1.4 %collective-permute-start.2 = (f32[128,256]{1,0:T(8,128)S(1)}, f32[128,256]{1,0:T(8,128)S(1)}, u32[]{:S(2)}, u32[]{:S(2)}) collective-permute-start(f32[128,256]{1,0:T(8,128)S(1)} %add.15), channel_id=1, source_target_pairs={{0,1},{1,0},{2,3},{3,2},{4,5},{5,4},{6,7},{7,6},{8,9},{9,8},{10,11... | collective-permute-start | bytes 393224 | tf_op jit(solution)/shard_map/ppermute | solution.py:103
  27.5 9.4 %collective-permute-start.3 = (f32[128,256]{1,0:T(8,128)S(1)}, f32[128,256]{1,0:T(8,128)S(1)}, u32[]{:S(2)}, u32[]{:S(2)}) collective-permute-start(f32[128,256]{1,0:T(8,128)S(1)} %add.16), channel_id=1, source_target_pairs={{0,2},{1,3},{2,0},{3,1},{4,6},{5,7},{6,4},{7,5},{8,10},{9,11},{10,... | collective-permute-start | bytes 393224 | tf_op jit(solution)/shard_map/ppermute | solution.py:104

commit v2 on v1

v2 whole, which is shorter than its diff:
```python
import functools

import jax
import jax.numpy as jnp
from jax import lax
from jax.experimental import pallas as pl
from jax.experimental.pallas import tpu as pltpu
from jax.sharding import PartitionSpec as P

CHUNK = 1024
DEPTH = 6


def split(value):
    high = value.astype(jnp.bfloat16)
    low = (value - high.astype(jnp.float32)).astype(jnp.bfloat16)
    return high, low


def dot(a, b):
    return jnp.dot(a, b, preferred_element_type=jnp.float32)


def pieces(depth):
    sizes = []
    left = depth
    while left > CHUNK:
        sizes.append(CHUNK)
        left -= CHUNK
    while left > 256 and left % 256 == 0:
        sizes.append(left // 2)
        left -= left // 2
    sizes.append(left)
    spans, start = [], 0
    for size in sizes:
        spans.append((start, size))
        start += size
    return spans


def matmul_kernel(spans, pick, a_hbm, b_hbm, first, second, a_buf, b_buf, sems):
    def copies(step):
        where = pl.ds(*spans[step])
        return (
            pltpu.make_async_copy(a_hbm.at[:, where], a_buf.at[:, where], sems.at[0, step]),
            pltpu.make_async_copy(b_hbm.at[where, :], b_buf.at[where, :], sems.at[1, step]),
        )

    def start(step):
        for copy in copies(step):
            copy.start()

    steps = len(spans)
    for step in range(min(DEPTH, steps)):
        start(step)
    half = a_hbm.shape[0] // 2
    totals = [jnp.zeros(first.shape, jnp.float32) for _ in range(2)]
    for step, (begin, size) in enumerate(spans):
        for copy in copies(step):
            copy.wait()
        if step + DEPTH < steps:
            start(step + DEPTH)
        b_high, b_low = split(b_buf[begin : begin + size])
        for side in range(2):
            a_high, a_low = split(a_buf[side * half : (side + 1) * half, begin : begin + size])
            totals[side] += dot(a_high, b_high) + dot(a_high, b_low) + dot(a_low, b_high)
    chosen = pick()

    @pl.when(chosen == 0)
    def _():
        first[...] = totals[0]
        second[...] = totals[1]

    @pl.when(chosen != 0)
    def _():
        first[...] = totals[1]
        second[...] = totals[0]


def matmul(a, b, pick):
    rows, depth = a.shape
    columns = b.shape[1]
    spans = pieces(depth)
    half = pltpu.VMEM((rows // 2, columns), jnp.float32)
    return pl.pallas_call(
        functools.partial(matmul_kernel, spans, pick),
        out_shape=(half, half),
        in_specs=[pl.BlockSpec(memory_space=pl.ANY)] * 2,
        out_specs=(pl.BlockSpec(memory_space=pltpu.VMEM),) * 2,
        scratch_shapes=[
            pltpu.VMEM((rows, depth), jnp.float32),
            pltpu.VMEM((depth, columns), jnp.float32),
            pltpu.SemaphoreType.DMA((2, len(spans))),
        ],
        compiler_params=pltpu.CompilerParams(vmem_limit_bytes=48 * 2**20),
    )(a, b)


def permute(value, n_row, n_col, target):
    pairs = []
    for r in range(n_row):
        for c in range(n_col):
            to_r, to_c = target(r, c)
            pairs.append((r * n_col + c, to_r * n_col + to_c))
    return lax.ppermute(value, ("row", "col"), pairs)


def general(operator, basis, n_row, n_col):
    partial = jnp.concatenate(matmul(operator, basis, lambda: 0), 0)
    group = n_row // n_col
    out_rows = partial.shape[0] // group
    summed = lax.psum(partial, "row")
    row = lax.axis_index("row")
    picked = lax.dynamic_slice_in_dim(summed, row % group * out_rows, out_rows, 0)
    kept = jnp.where(lax.axis_index("col") == row // group, picked, 0)
    return lax.psum(kept, "col")


def square(operator, basis, n_row, n_col):
    def side(r, c):
        return (r // 2) ^ (c // 2)

    def core_first(r, c):
        return (r ^ 1) % 2

    def core_second(r, c):
        return (r ^ 1) % 2

    def pick():
        return side(lax.axis_index("row"), lax.axis_index("col"))

    one, two = matmul(operator, basis, pick)
    one = permute(one, n_row, n_col, lambda r, c: (c, 2 * side(r, c) + core_first(r, c)))
    two = permute(two, n_row, n_col, lambda r, c: (c, 2 * (1 - side(r, c)) + core_second(r, c)))
    mine = two + one
    mine = mine + lax.ppermute(mine, "col", [(c, c ^ 1) for c in range(n_col)])
    other = lax.ppermute(mine, "col", [(c, c ^ 2) for c in range(n_col)])
    left = lax.axis_index("col") < 2
    return jnp.concatenate([jnp.where(left, mine, other), jnp.where(left, other, mine)], 0)


def shards(operator, basis):
    n_row, n_col = lax.axis_size("row"), lax.axis_size("col")
    if n_row == 4 and n_col == 4:
        return square(operator, basis, n_row, n_col)
    return general(operator, basis, n_row, n_col)


def solution(mesh):
    in_specs = (P(("reach", "col"), "row"), P(("reach", "row"), None))
    out_specs = P(("reach", "row"), None)
    return jax.shard_map(shards, mesh=mesh, in_specs=in_specs, out_specs=out_specs, check_vma=False)
```

time: 37.8 us -> 35.3 us (0.934)
  waiting for transfers between devices: 14.1 us -> 12.4 us
  local copies, waits for them, and re-layouts: 0.99 us -> 0 us
  starting transfers between devices: 9.33 us -> 10.2 us
  Pallas kernels: 12.4 us -> 11.7 us
    ppermute x1, starting transfers between devices: 0.07 us -> 2.93 us  [square(): mine = mine + lax.ppermute(mine, 'col', [(c, c ^ 1) for c in range(n_col)])]
    ppermute x1, starting transfers between devices: 5.61 us -> 3.69 us  [square(): other = lax.ppermute(mine, 'col', [(c, c ^ 2) for c in range(n_col)])]
    ppermute x2, waiting for transfers between devices: 9 us -> 7.41 us  [permute(): return lax.ppermute(value, ('row', 'col'), pairs)]
    dynamic_slice x1 -> x0, local copies, waits for them, and re-layouts: 0.99 us -> none  [square(): far = lax.dynamic_slice_in_dim(partial, (1 - side) * half, half, 0)]
    pallas_call x1, Pallas kernels: 12.4 us -> 11.7 us  [matmul(): pl.pallas_call(functools.partial(matmul_kernel, spans, pick), out_shape=(...]
  transfers between devices with their start and end apart: 4 -> 4, of which waited for: 3 -> 4; matrix products, arithmetic and copies ran while one was open for 0% -> 0% of each run, Pallas kernels for 0% -> 0%
where the time goes in v2:
time: 35.3 us; the launch traced here: 35.2 us
  waiting for transfers between devices  12.4 us (35%)
  Pallas kernels  11.7 us (33%)
  starting transfers between devices  10.2 us (29%)
  other arithmetic  0.77 us (2%)
    pallas_call x1, Pallas kernels, matmul(): pl.pallas_call(functools.partial(matmul_kernel, spans, pick), out_shape=(...  11.7 us
    ppermute x2, waiting for transfers between devices, permute(): return lax.ppermute(value, ('row', 'col'), pairs)  7.41 us
    ppermute x1, waiting for transfers between devices, square(): other = lax.ppermute(mine, 'col', [(c, c ^ 2) for c in range(n_col)])  4.01 us
    ppermute x1, starting transfers between devices, square(): other = lax.ppermute(mine, 'col', [(c, c ^ 2) for c in range(n_col)])  3.69 us
    ppermute x2, starting transfers between devices, permute(): return lax.ppermute(value, ('row', 'col'), pairs)  3.6 us
    ppermute x1, starting transfers between devices, square(): mine = mine + lax.ppermute(mine, 'col', [(c, c ^ 1) for c in range(n_col)])  2.93 us
    ppermute x1, waiting for transfers between devices, square(): mine = mine + lax.ppermute(mine, 'col', [(c, c ^ 1) for c in range(n_col)])  0.99 us
    concatenate x1, other arithmetic, square(): jnp.concatenate([jnp.where(left, mine, other), jnp.where(left, other, min...  0.72 us
  transfers between devices with their start and end apart: 4, of which 4 were waited for; matrix products, arithmetic and copies ran while one was open for 0% of the time, Pallas kernels for 0%

profile of v2, /device:TPU:0, one launch (start us, length us, event | category | flops | bytes accessed | tf_op | source)
XLA Modules:
  0.0 35.2 jit_solution(11097649558679408802)
XLA Ops:
  0.0 11.7 %shard_map.28 = (f32[128,256]{1,0:T(8,128)S(1)}, f32[128,256]{1,0:T(8,128)S(1)}) custom-call(f32[256,16384]{1,0:T(8,128)} %a_hbm.1, f32[16384,256]{1,0:T(8,128)} %b_hbm.1), custom_call_target="tpu_custom_call" | custom-call | tf_op jit(solution)/shard_map/pallas_call | solution.py:85
  11.7 2.5 %collective-permute-start = (f32[128,256]{1,0:T(8,128)S(1)}, f32[128,256]{1,0:T(8,128)S(1)}, u32[]{:S(2)}, u32[]{:S(2)}) collective-permute-start(f32[128,256]{1,0:T(8,128)S(1)} %get-tuple-element.7), channel_id=1, source_target_pairs={{0,3},{1,7},{2,9},{3,13},{4,2},{5,6},{6,8},{7,12},{8,1},{9,5},{10,... | collective-permute-start | bytes 393224 | tf_op jit(solution)/shard_map/ppermute | solution.py:105
  14.2 1.1 %collective-permute-start.1 = (f32[128,256]{1,0:T(8,128)S(1)}, f32[128,256]{1,0:T(8,128)S(1)}, u32[]{:S(2)}, u32[]{:S(2)}) collective-permute-start(f32[128,256]{1,0:T(8,128)S(1)} %get-tuple-element.8), channel_id=1, source_target_pairs={{0,1},{1,5},{2,11},{3,15},{4,0},{5,4},{6,10},{7,14},{8,3},{9,7},{1... | collective-permute-start | bytes 393224 | tf_op jit(solution)/shard_map/ppermute | solution.py:105
  15.3 6.0 %collective-permute-done = f32[128,256]{1,0:T(8,128)S(1)} collective-permute-done((f32[128,256]{1,0:T(8,128)S(1)}, f32[128,256]{1,0:T(8,128)S(1)}, u32[]{:S(2)}, u32[]{:S(2)}) %collective-permute-start) | collective-permute-done | bytes 131104 | tf_op jit(solution)/shard_map/ppermute | solution.py:105
  21.3 1.4 %collective-permute-done.1 = f32[128,256]{1,0:T(8,128)S(1)} collective-permute-done((f32[128,256]{1,0:T(8,128)S(1)}, f32[128,256]{1,0:T(8,128)S(1)}, u32[]{:S(2)}, u32[]{:S(2)}) %collective-permute-start.1) | collective-permute-done | bytes 131104 | tf_op jit(solution)/shard_map/ppermute | solution.py:105
  22.8 2.9 %collective-permute-start.2 = (f32[128,256]{1,0:T(8,128)S(1)}, f32[128,256]{1,0:T(8,128)S(1)}, u32[]{:S(2)}, u32[]{:S(2)}) collective-permute-start(f32[128,256]{1,0:T(8,128)S(1)} %add.6), channel_id=1, source_target_pairs={{0,1},{1,0},{2,3},{3,2},{4,5},{5,4},{6,7},{7,6},{8,9},{9,8},{10,11... | collective-permute-start | bytes 393224 | tf_op jit(solution)/shard_map/ppermute | solution.py:136
  25.7 1.0 %collective-permute-done.2 = f32[128,256]{1,0:T(8,128)S(1)} collective-permute-done((f32[128,256]{1,0:T(8,128)S(1)}, f32[128,256]{1,0:T(8,128)S(1)}, u32[]{:S(2)}, u32[]{:S(2)}) %collective-permute-start.2) | collective-permute-done | bytes 131104 | tf_op jit(solution)/shard_map/ppermute | solution.py:136
  26.7 3.7 %collective-permute-start.3 = (f32[128,256]{1,0:T(8,128)S(1)}, f32[128,256]{1,0:T(8,128)S(1)}, u32[]{:S(2)}, u32[]{:S(2)}) collective-permute-start(f32[128,256]{1,0:T(8,128)S(1)} %add.7), channel_id=1, source_target_pairs={{0,2},{1,3},{2,0},{3,1},{4,6},{5,7},{6,4},{7,5},{8,10},{9,11},{10,... | collective-permute-start | bytes 393224 | tf_op jit(solution)/shard_map/ppermute | solution.py:137
  30.4 4.0 %collective-permute-done.3 = f32[128,256]{1,0:T(8,128)S(1)} collective-permute-done((f32[128,256]{1,0:T(8,128)S(1)}, f32[128,256]{1,0:T(8,128)S(1)}, u32[]{:S(2)}, u32[]{:S(2)}) %collective-permute-start.3) | collective-permute-done | bytes 131104 | tf_op jit(solution)/shard_map/ppermute | solution.py:137
  34.4 0.7 %pad_maximum_fusion = f32[256,256]{1,0:T(8,128)} fusion(f32[128,256]{1,0:T(8,128)S(1)} %get-tuple-element.10, f32[128,256]{1,0:T(8,128)S(1)} %get-tuple-element.9), kind=kLoop, calls=%fused_computation | loop fusion | flops 65536 | bytes 524288 | tf_op jit(solution)/shard_map/concatenate | solution.py:139
  (3 shorter events, 0.1 us)
Async XLA Ops:
  11.7 9.6 %collective-permute-start = (f32[128,256]{1,0:T(8,128)S(1)}, f32[128,256]{1,0:T(8,128)S(1)}, u32[]{:S(2)}, u32[]{:S(2)}) collective-permute-start(f32[128,256]{1,0:T(8,128)S(1)} %get-tuple-element.7), channel_id=1, source_target_pairs={{0,3},{1,7},{2,9},{3,13},{4,2},{5,6},{6,8},{7,12},{8,1},{9,5},{10,... | collective-permute-start | bytes 393224 | tf_op jit(solution)/shard_map/ppermute | solution.py:105
  14.2 8.5 %collective-permute-start.1 = (f32[128,256]{1,0:T(8,128)S(1)}, f32[128,256]{1,0:T(8,128)S(1)}, u32[]{:S(2)}, u32[]{:S(2)}) collective-permute-start(f32[128,256]{1,0:T(8,128)S(1)} %get-tuple-element.8), channel_id=1, source_target_pairs={{0,1},{1,5},{2,11},{3,15},{4,0},{5,4},{6,10},{7,14},{8,3},{9,7},{1... | collective-permute-start | bytes 393224 | tf_op jit(solution)/shard_map/ppermute | solution.py:105
  22.8 3.9 %collective-permute-start.2 = (f32[128,256]{1,0:T(8,128)S(1)}, f32[128,256]{1,0:T(8,128)S(1)}, u32[]{:S(2)}, u32[]{:S(2)}) collective-permute-start(f32[128,256]{1,0:T(8,128)S(1)} %add.6), channel_id=1, source_target_pairs={{0,1},{1,0},{2,3},{3,2},{4,5},{5,4},{6,7},{7,6},{8,9},{9,8},{10,11... | collective-permute-start | bytes 393224 | tf_op jit(solution)/shard_map/ppermute | solution.py:136
  26.7 7.7 %collective-permute-start.3 = (f32[128,256]{1,0:T(8,128)S(1)}, f32[128,256]{1,0:T(8,128)S(1)}, u32[]{:S(2)}, u32[]{:S(2)}) collective-permute-start(f32[128,256]{1,0:T(8,128)S(1)} %add.7), channel_id=1, source_target_pairs={{0,2},{1,3},{2,0},{3,1},{4,6},{5,7},{6,4},{7,5},{8,10},{9,11},{10,... | collective-permute-start | bytes 393224 | tf_op jit(solution)/shard_map/ppermute | solution.py:137

commit v3 on v2

--- a/solution.py
+++ b/solution.py
@@ -38,7 +38,7 @@
     return spans
 
 
-def matmul_kernel(spans, pick, a_hbm, b_hbm, first, second, a_buf, b_buf, sems):
+def matmul_kernel(spans, pick, a_hbm, b_hbm, first, second, third, a_buf, b_buf, sems):
     def copies(step):
         where = pl.ds(*spans[step])
         return (
@@ -66,15 +66,18 @@
             totals[side] += dot(a_high, b_high) + dot(a_high, b_low) + dot(a_low, b_high)
     chosen = pick()
 
+    def put(whole, cut):
+        first[...] = whole
+        second[...] = cut[: second.shape[0]]
+        third[...] = cut[second.shape[0] :]
+
     @pl.when(chosen == 0)
     def _():
-        first[...] = totals[0]
-        second[...] = totals[1]
+        put(totals[0], totals[1])
 
     @pl.when(chosen != 0)
     def _():
-        first[...] = totals[1]
-        second[...] = totals[0]
+        put(totals[1], totals[0])
 
 
 def matmul(a, b, pick):
@@ -82,11 +85,14 @@
     columns = b.shape[1]
     spans = pieces(depth)
     half = pltpu.VMEM((rows // 2, columns), jnp.float32)
+    relayed = rows // 2 // 2
+    direct = pltpu.VMEM((rows // 2 - relayed, columns), jnp.float32)
+    relay = pltpu.VMEM((relayed, columns), jnp.float32)
     return pl.pallas_call(
         functools.partial(matmul_kernel, spans, pick),
-        out_shape=(half, half),
+        out_shape=(half, direct, relay),
         in_specs=[pl.BlockSpec(memory_space=pl.ANY)] * 2,
-        out_specs=(pl.BlockSpec(memory_space=pltpu.VMEM),) * 2,
+        out_specs=(pl.BlockSpec(memory_space=pltpu.VMEM),) * 3,
         scratch_shapes=[
             pltpu.VMEM((rows, depth), jnp.float32),
             pltpu.VMEM((depth, columns), jnp.float32),
@@ -117,9 +123,6 @@
 
 
 def square(operator, basis, n_row, n_col):
-    def side(r, c):
-        return (r // 2) ^ (c // 2)
-
     def core_first(r, c):
         return (r ^ 1) % 2
 
@@ -127,12 +130,14 @@
         return (r ^ 1) % 2
 
     def pick():
-        return side(lax.axis_index("row"), lax.axis_index("col"))
+        return 1 - lax.axis_index("row") // 2
 
-    one, two = matmul(operator, basis, pick)
-    one = permute(one, n_row, n_col, lambda r, c: (c, 2 * side(r, c) + core_first(r, c)))
-    two = permute(two, n_row, n_col, lambda r, c: (c, 2 * (1 - side(r, c)) + core_second(r, c)))
-    mine = two + one
+    first, direct, relay = matmul(operator, basis, pick)
+    relay = lax.ppermute(relay, "col", [(c, c ^ 2) for c in range(n_col)])
+    first = permute(first, n_row, n_col, lambda r, c: (c, 2 * (1 - r // 2) + core_first(r, c)))
+    direct = permute(direct, n_row, n_col, lambda r, c: (c, 2 * (r // 2) + core_second(r, c)))
+    relay = permute(relay, n_row, n_col, lambda r, c: (c ^ 2, 2 * (r // 2) + core_second(r, c ^ 2)))
+    mine = first + jnp.concatenate([direct, relay], 0)
     mine = mine + lax.ppermute(mine, "col", [(c, c ^ 1) for c in range(n_col)])
     other = lax.ppermute(mine, "col", [(c, c ^ 2) for c in range(n_col)])
     left = lax.axis_index("col") < 2

time: 35.3 us -> 33.7 us (0.955)
  starting transfers between devices: 10.2 us -> 8.56 us
    ppermute x0 -> x1, starting transfers between devices: none -> 3 us  [square(): relay = lax.ppermute(relay, 'col', [(c, c ^ 2) for c in range(n_col)])]
    ppermute x1, starting transfers between devices: 2.93 us -> 0.18 us  [square(): mine = mine + lax.ppermute(mine, 'col', [(c, c ^ 1) for c in range(n_col)])]
    ppermute x1, starting transfers between devices: 3.69 us -> 1.75 us  [square(): other = lax.ppermute(mine, 'col', [(c, c ^ 2) for c in range(n_col)])]
    ppermute x2 -> x3, waiting for transfers between devices: 7.41 us -> 5.81 us  [permute(): return lax.ppermute(value, ('row', 'col'), pairs)]
    ppermute x0 -> x1, waiting for transfers between devices: none -> 1.41 us  [square(): relay = lax.ppermute(relay, 'col', [(c, c ^ 2) for c in range(n_col)])]
    ppermute x2 -> x3, starting transfers between devices: 3.6 us -> 3.63 us  [permute(): return lax.ppermute(value, ('row', 'col'), pairs)]
  transfers between devices with their start and end apart: 4 -> 6, of which waited for: 4 -> 5; matrix products, arithmetic and copies ran while one was open for 0% -> 0% of each run, Pallas kernels for 0% -> 0%
where the time goes in v3:
time: 33.7 us; the launch traced here: 33.6 us
  waiting for transfers between devices  12.5 us (37%)
  Pallas kernels  11.8 us (35%)
  starting transfers between devices  8.56 us (25%)
  other arithmetic  0.77 us (2%)
    pallas_call x1, Pallas kernels, matmul(): pl.pallas_call(functools.partial(matmul_kernel, spans, pick), out_shape=(...  11.8 us
    ppermute x3, waiting for transfers between devices, permute(): return lax.ppermute(value, ('row', 'col'), pairs)  5.81 us
    ppermute x1, waiting for transfers between devices, square(): other = lax.ppermute(mine, 'col', [(c, c ^ 2) for c in range(n_col)])  4.01 us
    ppermute x3, starting transfers between devices, permute(): return lax.ppermute(value, ('row', 'col'), pairs)  3.63 us
    ppermute x1, starting transfers between devices, square(): relay = lax.ppermute(relay, 'col', [(c, c ^ 2) for c in range(n_col)])  3 us
    ppermute x1, starting transfers between devices, square(): other = lax.ppermute(mine, 'col', [(c, c ^ 2) for c in range(n_col)])  1.75 us
    ppermute x1, waiting for transfers between devices, square(): relay = lax.ppermute(relay, 'col', [(c, c ^ 2) for c in range(n_col)])  1.41 us
    ppermute x1, waiting for transfers between devices, square(): mine = mine + lax.ppermute(mine, 'col', [(c, c ^ 1) for c in range(n_col)])  1.24 us
  transfers between devices with their start and end apart: 6, of which 5 were waited for; matrix products, arithmetic and copies ran while one was open for 0% of the time, Pallas kernels for 0%

profile of v3, /device:TPU:0, one launch (start us, length us, event | category | flops | bytes accessed | tf_op | source)
XLA Modules:
  0.0 33.6 jit_solution(7245610339297124459)
XLA Ops:
  0.0 11.8 %shard_map.28 = (f32[128,256]{1,0:T(8,128)S(1)}, f32[64,256]{1,0:T(8,128)S(1)}, f32[64,256]{1,0:T(8,128)S(1)}) custom-call(f32[256,16384]{1,0:T(8,128)} %a_hbm.1, f32[16384,256]{1,0:T(8,128)} %b_hbm.1), custom_call_target="tpu_custom_call" | custom-call | tf_op jit(solution)/shard_map/pallas_call | solution.py:91
  11.8 3.0 %collective-permute-start.2 = (f32[64,256]{1,0:T(8,128)S(1)}, f32[64,256]{1,0:T(8,128)S(1)}, u32[]{:S(2)}, u32[]{:S(2)}) collective-permute-start(f32[64,256]{1,0:T(8,128)S(1)} %get-tuple-element.10), channel_id=1, source_target_pairs={{0,2},{1,3},{2,0},{3,1},{4,6},{5,7},{6,4},{7,5},{8,10},{9,11},{10,... | collective-permute-start | bytes 196616 | tf_op jit(solution)/shard_map/ppermute | solution.py:136
  14.8 0.0 collective-permute-start
  14.8 0.8 %collective-permute-start.1 = (f32[64,256]{1,0:T(8,128)S(1)}, f32[64,256]{1,0:T(8,128)S(1)}, u32[]{:S(2)}, u32[]{:S(2)}) collective-permute-start(f32[64,256]{1,0:T(8,128)S(1)} %get-tuple-element.9), channel_id=1, source_target_pairs={{0,1},{1,5},{2,9},{3,13},{4,0},{5,4},{6,8},{7,12},{8,3},{9,7},{10,... | collective-permute-start | bytes 196616 | tf_op jit(solution)/shard_map/ppermute | solution.py:111
  15.6 1.4 %collective-permute-done.2 = f32[64,256]{1,0:T(8,128)S(1)} collective-permute-done((f32[64,256]{1,0:T(8,128)S(1)}, f32[64,256]{1,0:T(8,128)S(1)}, u32[]{:S(2)}, u32[]{:S(2)}) %collective-permute-start.2) | collective-permute-done | bytes 65568 | tf_op jit(solution)/shard_map/ppermute | solution.py:136
  17.0 2.8 %collective-permute-start.3 = (f32[64,256]{1,0:T(8,128)S(1)}, f32[64,256]{1,0:T(8,128)S(1)}, u32[]{:S(2)}, u32[]{:S(2)}) collective-permute-start(f32[64,256]{1,0:T(8,128)S(1)} %collective-permute-done.2), channel_id=1, source_target_pairs={{0,9},{1,13},{2,1},{3,5},{4,8},{5,12},{6,0},{7,4},{8,11},{9,15},{1... | collective-permute-start | bytes 196616 | tf_op jit(solution)/shard_map/ppermute | solution.py:111
  19.8 1.0 %collective-permute-done.1 = f32[64,256]{1,0:T(8,128)S(1)} collective-permute-done((f32[64,256]{1,0:T(8,128)S(1)}, f32[64,256]{1,0:T(8,128)S(1)}, u32[]{:S(2)}, u32[]{:S(2)}) %collective-permute-start.1) | collective-permute-done | bytes 65568 | tf_op jit(solution)/shard_map/ppermute | solution.py:111
  20.8 4.8 %collective-permute-done.3 = f32[64,256]{1,0:T(8,128)S(1)} collective-permute-done((f32[64,256]{1,0:T(8,128)S(1)}, f32[64,256]{1,0:T(8,128)S(1)}, u32[]{:S(2)}, u32[]{:S(2)}) %collective-permute-start.3) | collective-permute-done | bytes 65568 | tf_op jit(solution)/shard_map/ppermute | solution.py:111
  25.6 0.0 collective-permute-done
  25.6 0.2 collective-permute-start.4
  25.8 1.2 %collective-permute-done.4 = f32[128,256]{1,0:T(8,128)S(1)} collective-permute-done((f32[128,256]{1,0:T(8,128)S(1)}, f32[128,256]{1,0:T(8,128)S(1)}, u32[]{:S(2)}, u32[]{:S(2)}) %collective-permute-start.4) | collective-permute-done | bytes 131104 | tf_op jit(solution)/shard_map/ppermute | solution.py:141
  27.1 1.8 %collective-permute-start.5 = (f32[128,256]{1,0:T(8,128)S(1)}, f32[128,256]{1,0:T(8,128)S(1)}, u32[]{:S(2)}, u32[]{:S(2)}) collective-permute-start(f32[128,256]{1,0:T(8,128)S(1)} %add.7), channel_id=1, source_target_pairs={{0,2},{1,3},{2,0},{3,1},{4,6},{5,7},{6,4},{7,5},{8,10},{9,11},{10,... | collective-permute-start | bytes 393224 | tf_op jit(solution)/shard_map/ppermute | solution.py:142
  28.8 4.0 %collective-permute-done.5 = f32[128,256]{1,0:T(8,128)S(1)} collective-permute-done((f32[128,256]{1,0:T(8,128)S(1)}, f32[128,256]{1,0:T(8,128)S(1)}, u32[]{:S(2)}, u32[]{:S(2)}) %collective-permute-start.5) | collective-permute-done | bytes 131104 | tf_op jit(solution)/shard_map/ppermute | solution.py:142
  32.9 0.7 %pad_maximum_fusion = f32[256,256]{1,0:T(8,128)} fusion(f32[128,256]{1,0:T(8,128)S(1)} %get-tuple-element.12, f32[128,256]{1,0:T(8,128)S(1)} %get-tuple-element.11), kind=kLoop, calls=%fused_computation | loop fusion | flops 65536 | bytes 524288 | tf_op jit(solution)/shard_map/concatenate | solution.py:144
  (3 shorter events, 0.1 us)
Async XLA Ops:
  11.8 5.2 %collective-permute-start.2 = (f32[64,256]{1,0:T(8,128)S(1)}, f32[64,256]{1,0:T(8,128)S(1)}, u32[]{:S(2)}, u32[]{:S(2)}) collective-permute-start(f32[64,256]{1,0:T(8,128)S(1)} %get-tuple-element.10), channel_id=1, source_target_pairs={{0,2},{1,3},{2,0},{3,1},{4,6},{5,7},{6,4},{7,5},{8,10},{9,11},{10,... | collective-permute-start | bytes 196616 | tf_op jit(solution)/shard_map/ppermute | solution.py:136
  14.8 10.9 %collective-permute-start = (f32[128,256]{1,0:T(8,128)S(1)}, f32[128,256]{1,0:T(8,128)S(1)}, u32[]{:S(2)}, u32[]{:S(2)}) collective-permute-start(f32[128,256]{1,0:T(8,128)S(1)} %get-tuple-element.8), channel_id=1, source_target_pairs={{0,3},{1,7},{2,11},{3,15},{4,2},{5,6},{6,10},{7,14},{8,1},{9,5},{1... | collective-permute-start | bytes 393224 | tf_op jit(solution)/shard_map/ppermute | solution.py:111
  14.8 6.0 %collective-permute-start.1 = (f32[64,256]{1,0:T(8,128)S(1)}, f32[64,256]{1,0:T(8,128)S(1)}, u32[]{:S(2)}, u32[]{:S(2)}) collective-permute-start(f32[64,256]{1,0:T(8,128)S(1)} %get-tuple-element.9), channel_id=1, source_target_pairs={{0,1},{1,5},{2,9},{3,13},{4,0},{5,4},{6,8},{7,12},{8,3},{9,7},{10,... | collective-permute-start | bytes 196616 | tf_op jit(solution)/shard_map/ppermute | solution.py:111
  17.0 8.6 %collective-permute-start.3 = (f32[64,256]{1,0:T(8,128)S(1)}, f32[64,256]{1,0:T(8,128)S(1)}, u32[]{:S(2)}, u32[]{:S(2)}) collective-permute-start(f32[64,256]{1,0:T(8,128)S(1)} %collective-permute-done.2), channel_id=1, source_target_pairs={{0,9},{1,13},{2,1},{3,5},{4,8},{5,12},{6,0},{7,4},{8,11},{9,15},{1... | collective-permute-start | bytes 196616 | tf_op jit(solution)/shard_map/ppermute | solution.py:111
  25.6 1.4 %collective-permute-start.4 = (f32[128,256]{1,0:T(8,128)S(1)}, f32[128,256]{1,0:T(8,128)S(1)}, u32[]{:S(2)}, u32[]{:S(2)}) collective-permute-start(f32[128,256]{1,0:T(8,128)S(1)} %maximum_add_fusion), channel_id=1, source_target_pairs={{0,1},{1,0},{2,3},{3,2},{4,5},{5,4},{6,7},{7,6},{8,9},{9,8},{10,11... | collective-permute-start | bytes 393224 | tf_op jit(solution)/shard_map/ppermute | solution.py:141
  27.1 5.8 %collective-permute-start.5 = (f32[128,256]{1,0:T(8,128)S(1)}, f32[128,256]{1,0:T(8,128)S(1)}, u32[]{:S(2)}, u32[]{:S(2)}) collective-permute-start(f32[128,256]{1,0:T(8,128)S(1)} %add.7), channel_id=1, source_target_pairs={{0,2},{1,3},{2,0},{3,1},{4,6},{5,7},{6,4},{7,5},{8,10},{9,11},{10,... | collective-permute-start | bytes 393224 | tf_op jit(solution)/shard_map/ppermute | solution.py:142

commit v4 on v3

--- a/solution.py
+++ b/solution.py
@@ -38,7 +38,7 @@
     return spans
 
 
-def matmul_kernel(spans, pick, a_hbm, b_hbm, first, second, third, a_buf, b_buf, sems):
+def matmul_kernel(spans, pick, a_hbm, b_hbm, early, late, second, third, a_buf, b_buf, sems):
     def copies(step):
         where = pl.ds(*spans[step])
         return (
@@ -54,7 +54,7 @@
     for step in range(min(DEPTH, steps)):
         start(step)
     half = a_hbm.shape[0] // 2
-    totals = [jnp.zeros(first.shape, jnp.float32) for _ in range(2)]
+    totals = [jnp.zeros((half, early.shape[1]), jnp.float32) for _ in range(2)]
     for step, (begin, size) in enumerate(spans):
         for copy in copies(step):
             copy.wait()
@@ -67,7 +67,8 @@
     chosen = pick()
 
     def put(whole, cut):
-        first[...] = whole
+        early[...] = whole[: early.shape[0]]
+        late[...] = whole[early.shape[0] :]
         second[...] = cut[: second.shape[0]]
         third[...] = cut[second.shape[0] :]
 
@@ -84,15 +85,12 @@
     rows, depth = a.shape
     columns = b.shape[1]
     spans = pieces(depth)
-    half = pltpu.VMEM((rows // 2, columns), jnp.float32)
-    relayed = rows // 2 // 2
-    direct = pltpu.VMEM((rows // 2 - relayed, columns), jnp.float32)
-    relay = pltpu.VMEM((relayed, columns), jnp.float32)
+    quarter = pltpu.VMEM((rows // 4, columns), jnp.float32)
     return pl.pallas_call(
         functools.partial(matmul_kernel, spans, pick),
-        out_shape=(half, direct, relay),
+        out_shape=(quarter,) * 4,
         in_specs=[pl.BlockSpec(memory_space=pl.ANY)] * 2,
-        out_specs=(pl.BlockSpec(memory_space=pltpu.VMEM),) * 3,
+        out_specs=(pl.BlockSpec(memory_space=pltpu.VMEM),) * 4,
         scratch_shapes=[
             pltpu.VMEM((rows, depth), jnp.float32),
             pltpu.VMEM((depth, columns), jnp.float32),
@@ -132,16 +130,26 @@
     def pick():
         return 1 - lax.axis_index("row") // 2
 
-    first, direct, relay = matmul(operator, basis, pick)
+    early, late, direct, relay = matmul(operator, basis, pick)
+
+    def near(value):
+        return permute(value, n_row, n_col, lambda r, c: (c, 2 * (1 - r // 2) + core_first(r, c)))
+
     relay = lax.ppermute(relay, "col", [(c, c ^ 2) for c in range(n_col)])
-    first = permute(first, n_row, n_col, lambda r, c: (c, 2 * (1 - r // 2) + core_first(r, c)))
+    relay, late = lax.optimization_barrier((relay, late))
+    early = near(early)
     direct = permute(direct, n_row, n_col, lambda r, c: (c, 2 * (r // 2) + core_second(r, c)))
     relay = permute(relay, n_row, n_col, lambda r, c: (c ^ 2, 2 * (r // 2) + core_second(r, c ^ 2)))
-    mine = first + jnp.concatenate([direct, relay], 0)
-    mine = mine + lax.ppermute(mine, "col", [(c, c ^ 1) for c in range(n_col)])
-    other = lax.ppermute(mine, "col", [(c, c ^ 2) for c in range(n_col)])
+    late = near(late)
+    mine, other = [], []
+    for part in (direct + early, relay + late):
+        part = part + lax.ppermute(part, "col", [(c, c ^ 1) for c in range(n_col)])
+        mine.append(part)
+        other.append(lax.ppermute(part, "col", [(c, c ^ 2) for c in range(n_col)]))
     left = lax.axis_index("col") < 2
-    return jnp.concatenate([jnp.where(left, mine, other), jnp.where(left, other, mine)], 0)
+    top = [jnp.where(left, m, o) for m, o in zip(mine, other)]
+    bottom = [jnp.where(left, o, m) for m, o in zip(mine, other)]
+    return jnp.concatenate(top + bottom, 0)
 
 
 def shards(operator, basis):

time: 33.7 us -> 33.1 us (0.982)
  waiting for transfers between devices: 12.5 us -> 8.63 us
  starting transfers between devices: 8.56 us -> 11.7 us
    ppermute x3 -> x4, starting transfers between devices: 3.63 us -> 5.51 us  [permute(): return lax.ppermute(value, ('row', 'col'), pairs)]
    ppermute x1, waiting for transfers between devices: 1.41 us -> 0.01 us  [square(): relay = lax.ppermute(relay, 'col', [(c, c ^ 2) for c in range(n_col)])]
    ppermute x3 -> x4, waiting for transfers between devices: 5.81 us -> 4.44 us  [permute(): return lax.ppermute(value, ('row', 'col'), pairs)]
    ppermute x2 -> x4, starting transfers between devices: 1.93 us -> 3.21 us  [the longest x2 1.63 us: square(): part = part + lax.ppermute(part, 'col', [(c, c ^ 1) for c in range(n_col)])]
    ppermute x2 -> x4, waiting for transfers between devices: 5.25 us -> 4.19 us  [the longest x2 3.61 us: square(): other.append(lax.ppermute(part, 'col', [(c, c ^ 2) for c in range(n_col)]))]
  transfers between devices with their start and end apart: 6 -> 9, of which waited for: 5 -> 6; matrix products, arithmetic and copies ran while one was open for 0% -> 0% of each run, Pallas kernels for 0% -> 0%
where the time goes in v4:
time: 33.1 us; the launch traced here: 32.9 us
  Pallas kernels  11.8 us (36%)
  starting transfers between devices  11.7 us (35%)
  waiting for transfers between devices  8.63 us (26%)
  other arithmetic  0.78 us (2%)
    pallas_call x1, Pallas kernels, matmul(): pl.pallas_call(functools.partial(matmul_kernel, spans, pick), out_shape=(...  11.8 us
    ppermute x4, starting transfers between devices, permute(): return lax.ppermute(value, ('row', 'col'), pairs)  5.51 us
    ppermute x4, waiting for transfers between devices, permute(): return lax.ppermute(value, ('row', 'col'), pairs)  4.44 us
    ppermute x2, waiting for transfers between devices, square(): other.append(lax.ppermute(part, 'col', [(c, c ^ 2) for c in range(n_col)]))  3.61 us
    ppermute x1, starting transfers between devices, square(): relay = lax.ppermute(relay, 'col', [(c, c ^ 2) for c in range(n_col)])  3 us
    ppermute x2, starting transfers between devices, square(): part = part + lax.ppermute(part, 'col', [(c, c ^ 1) for c in range(n_col)])  1.63 us
    ppermute x2, starting transfers between devices, square(): other.append(lax.ppermute(part, 'col', [(c, c ^ 2) for c in range(n_col)]))  1.58 us
    concatenate x1, other arithmetic, square(): return jnp.concatenate(top + bottom, 0)  0.72 us
  transfers between devices with their start and end apart: 9, of which 6 were waited for; matrix products, arithmetic and copies ran while one was open for 0% of the time, Pallas kernels for 0%

profile of v4, /device:TPU:0, one launch (start us, length us, event | category | flops | bytes accessed | tf_op | source)
XLA Modules:
  0.0 32.9 jit_solution(16897419379946895774)
XLA Ops:
  0.0 11.8 %shard_map.28 = (f32[64,256]{1,0:T(8,128)S(1)}, f32[64,256]{1,0:T(8,128)S(1)}, f32[64,256]{1,0:T(8,128)S(1)}, f32[64,256]{1,0:T(8,128)S(1)}) custom-call(f32[256,16384]{1,0:T(8,128)} %a_hbm.1, f32[16384,256]{1,0:T(8,128)} %b_hbm.1), custom_call_target="tpu_custom_call" | custom-call | tf_op jit(solution)/shard_map/pallas_call | solution.py:89
  11.8 3.0 %collective-permute-start.4 = (f32[64,256]{1,0:T(8,128)S(1)}, f32[64,256]{1,0:T(8,128)S(1)}, u32[]{:S(2)}, u32[]{:S(2)}) collective-permute-start(f32[64,256]{1,0:T(8,128)S(1)} %get-tuple-element.13), channel_id=1, source_target_pairs={{0,2},{1,3},{2,0},{3,1},{4,6},{5,7},{6,4},{7,5},{8,10},{9,11},{10,... | collective-permute-start | bytes 196616 | tf_op jit(solution)/shard_map/ppermute | solution.py:138
  14.8 0.0 collective-permute-start
  14.8 3.9 %collective-permute-start.1 = (f32[64,256]{1,0:T(8,128)S(1)}, f32[64,256]{1,0:T(8,128)S(1)}, u32[]{:S(2)}, u32[]{:S(2)}) collective-permute-start(f32[64,256]{1,0:T(8,128)S(1)} %get-tuple-element.12), channel_id=1, source_target_pairs={{0,3},{1,7},{2,11},{3,15},{4,2},{5,6},{6,10},{7,14},{8,1},{9,5},{1... | collective-permute-start | bytes 196616 | tf_op jit(solution)/shard_map/ppermute | solution.py:109
  18.7 0.0 collective-permute-done.4
  18.7 0.0 collective-permute-start.5
  18.7 1.6 %collective-permute-start.6 = (f32[64,256]{1,0:T(8,128)S(1)}, f32[64,256]{1,0:T(8,128)S(1)}, u32[]{:S(2)}, u32[]{:S(2)}) collective-permute-start(f32[64,256]{1,0:T(8,128)S(1)} %get-tuple-element.16), channel_id=1, source_target_pairs={{0,3},{1,7},{2,11},{3,15},{4,2},{5,6},{6,10},{7,14},{8,1},{9,5},{1... | collective-permute-start | bytes 196616 | tf_op jit(solution)/shard_map/ppermute | solution.py:109
  20.3 0.0 collective-permute-done
  20.3 2.3 %collective-permute-done.1 = f32[64,256]{1,0:T(8,128)S(1)} collective-permute-done((f32[64,256]{1,0:T(8,128)S(1)}, f32[64,256]{1,0:T(8,128)S(1)}, u32[]{:S(2)}, u32[]{:S(2)}) %collective-permute-start.1) | collective-permute-done | bytes 65568 | tf_op jit(solution)/shard_map/ppermute | solution.py:109
  22.6 1.4 %collective-permute-start.2 = (f32[64,256]{1,0:T(8,128)S(1)}, f32[64,256]{1,0:T(8,128)S(1)}, u32[]{:S(2)}, u32[]{:S(2)}) collective-permute-start(f32[64,256]{1,0:T(8,128)S(1)} %add.12), channel_id=1, source_target_pairs={{0,1},{1,0},{2,3},{3,2},{4,5},{5,4},{6,7},{7,6},{8,9},{9,8},{10,11... | collective-permute-start | bytes 196616 | tf_op jit(solution)/shard_map/ppermute | solution.py:146
  24.0 0.6 %collective-permute-done.5 = f32[64,256]{1,0:T(8,128)S(1)} collective-permute-done((f32[64,256]{1,0:T(8,128)S(1)}, f32[64,256]{1,0:T(8,128)S(1)}, u32[]{:S(2)}, u32[]{:S(2)}) %collective-permute-start.5) | collective-permute-done | bytes 65568 | tf_op jit(solution)/shard_map/ppermute | solution.py:109
  24.6 1.5 %collective-permute-done.6 = f32[64,256]{1,0:T(8,128)S(1)} collective-permute-done((f32[64,256]{1,0:T(8,128)S(1)}, f32[64,256]{1,0:T(8,128)S(1)}, u32[]{:S(2)}, u32[]{:S(2)}) %collective-permute-start.6) | collective-permute-done | bytes 65568 | tf_op jit(solution)/shard_map/ppermute | solution.py:109
  26.1 0.2 collective-permute-start.7
  26.4 0.0 collective-permute-done.2
  26.4 0.5 %collective-permute-start.3 = (f32[64,256]{1,0:T(8,128)S(1)}, f32[64,256]{1,0:T(8,128)S(1)}, u32[]{:S(2)}, u32[]{:S(2)}) collective-permute-start(f32[64,256]{1,0:T(8,128)S(1)} %add.13), channel_id=1, source_target_pairs={{0,2},{1,3},{2,0},{3,1},{4,6},{5,7},{6,4},{7,5},{8,10},{9,11},{10,... | collective-permute-start | bytes 196616 | tf_op jit(solution)/shard_map/ppermute | solution.py:148
  26.9 0.6 %collective-permute-done.7 = f32[64,256]{1,0:T(8,128)S(1)} collective-permute-done((f32[64,256]{1,0:T(8,128)S(1)}, f32[64,256]{1,0:T(8,128)S(1)}, u32[]{:S(2)}, u32[]{:S(2)}) %collective-permute-start.7) | collective-permute-done | bytes 65568 | tf_op jit(solution)/shard_map/ppermute | solution.py:146
  27.5 1.1 %collective-permute-start.8 = (f32[64,256]{1,0:T(8,128)S(1)}, f32[64,256]{1,0:T(8,128)S(1)}, u32[]{:S(2)}, u32[]{:S(2)}) collective-permute-start(f32[64,256]{1,0:T(8,128)S(1)} %add.15), channel_id=1, source_target_pairs={{0,2},{1,3},{2,0},{3,1},{4,6},{5,7},{6,4},{7,5},{8,10},{9,11},{10,... | collective-permute-start | bytes 196616 | tf_op jit(solution)/shard_map/ppermute | solution.py:148
  28.6 2.7 %collective-permute-done.3 = f32[64,256]{1,0:T(8,128)S(1)} collective-permute-done((f32[64,256]{1,0:T(8,128)S(1)}, f32[64,256]{1,0:T(8,128)S(1)}, u32[]{:S(2)}, u32[]{:S(2)}) %collective-permute-start.3) | collective-permute-done | bytes 65568 | tf_op jit(solution)/shard_map/ppermute | solution.py:148
  31.3 0.9 %collective-permute-done.8 = f32[64,256]{1,0:T(8,128)S(1)} collective-permute-done((f32[64,256]{1,0:T(8,128)S(1)}, f32[64,256]{1,0:T(8,128)S(1)}, u32[]{:S(2)}, u32[]{:S(2)}) %collective-permute-start.8) | collective-permute-done | bytes 65568 | tf_op jit(solution)/shard_map/ppermute | solution.py:148
  32.2 0.7 %pad_maximum_fusion = f32[256,256]{1,0:T(8,128)} fusion(f32[64,256]{1,0:T(8,128)S(1)} %get-tuple-element.20, f32[64,256]{1,0:T(8,128)S(1)} %get-tuple-element.18, f32[64,256]{1,0:T(8,128)S(1)} %get-tuple-element.19, f32[64,256]{1,0:T(8,128)S(1)} %get-tuple-element.17), kind=kLoop, calls=%fused_computation | loop fusion | flops 196608 | bytes 524288 | tf_op jit(solution)/shard_map/concatenate | solution.py:152
  (6 shorter events, 0.1 us)
Async XLA Ops:
  11.8 6.9 %collective-permute-start.4 = (f32[64,256]{1,0:T(8,128)S(1)}, f32[64,256]{1,0:T(8,128)S(1)}, u32[]{:S(2)}, u32[]{:S(2)}) collective-permute-start(f32[64,256]{1,0:T(8,128)S(1)} %get-tuple-element.13), channel_id=1, source_target_pairs={{0,2},{1,3},{2,0},{3,1},{4,6},{5,7},{6,4},{7,5},{8,10},{9,11},{10,... | collective-permute-start | bytes 196616 | tf_op jit(solution)/shard_map/ppermute | solution.py:138
  14.8 5.5 %collective-permute-start = (f32[64,256]{1,0:T(8,128)S(1)}, f32[64,256]{1,0:T(8,128)S(1)}, u32[]{:S(2)}, u32[]{:S(2)}) collective-permute-start(f32[64,256]{1,0:T(8,128)S(1)} %get-tuple-element.11), channel_id=1, source_target_pairs={{0,1},{1,5},{2,9},{3,13},{4,0},{5,4},{6,8},{7,12},{8,3},{9,7},{10,... | collective-permute-start | bytes 196616 | tf_op jit(solution)/shard_map/ppermute | solution.py:109
  14.8 7.8 %collective-permute-start.1 = (f32[64,256]{1,0:T(8,128)S(1)}, f32[64,256]{1,0:T(8,128)S(1)}, u32[]{:S(2)}, u32[]{:S(2)}) collective-permute-start(f32[64,256]{1,0:T(8,128)S(1)} %get-tuple-element.12), channel_id=1, source_target_pairs={{0,3},{1,7},{2,11},{3,15},{4,2},{5,6},{6,10},{7,14},{8,1},{9,5},{1... | collective-permute-start | bytes 196616 | tf_op jit(solution)/shard_map/ppermute | solution.py:109
  18.7 5.9 %collective-permute-start.5 = (f32[64,256]{1,0:T(8,128)S(1)}, f32[64,256]{1,0:T(8,128)S(1)}, u32[]{:S(2)}, u32[]{:S(2)}) collective-permute-start(f32[64,256]{1,0:T(8,128)S(1)} %collective-permute-done.4), channel_id=1, source_target_pairs={{0,9},{1,13},{2,1},{3,5},{4,8},{5,12},{6,0},{7,4},{8,11},{9,15},{1... | collective-permute-start | bytes 196616 | tf_op jit(solution)/shard_map/ppermute | solution.py:109
  18.7 7.4 %collective-permute-start.6 = (f32[64,256]{1,0:T(8,128)S(1)}, f32[64,256]{1,0:T(8,128)S(1)}, u32[]{:S(2)}, u32[]{:S(2)}) collective-permute-start(f32[64,256]{1,0:T(8,128)S(1)} %get-tuple-element.16), channel_id=1, source_target_pairs={{0,3},{1,7},{2,11},{3,15},{4,2},{5,6},{6,10},{7,14},{8,1},{9,5},{1... | collective-permute-start | bytes 196616 | tf_op jit(solution)/shard_map/ppermute | solution.py:109
  22.6 3.8 %collective-permute-start.2 = (f32[64,256]{1,0:T(8,128)S(1)}, f32[64,256]{1,0:T(8,128)S(1)}, u32[]{:S(2)}, u32[]{:S(2)}) collective-permute-start(f32[64,256]{1,0:T(8,128)S(1)} %add.12), channel_id=1, source_target_pairs={{0,1},{1,0},{2,3},{3,2},{4,5},{5,4},{6,7},{7,6},{8,9},{9,8},{10,11... | collective-permute-start | bytes 196616 | tf_op jit(solution)/shard_map/ppermute | solution.py:146
  26.1 1.3 %collective-permute-start.7 = (f32[64,256]{1,0:T(8,128)S(1)}, f32[64,256]{1,0:T(8,128)S(1)}, u32[]{:S(2)}, u32[]{:S(2)}) collective-permute-start(f32[64,256]{1,0:T(8,128)S(1)} %add.14), channel_id=1, source_target_pairs={{0,1},{1,0},{2,3},{3,2},{4,5},{5,4},{6,7},{7,6},{8,9},{9,8},{10,11... | collective-permute-start | bytes 196616 | tf_op jit(solution)/shard_map/ppermute | solution.py:146
  26.4 4.9 %collective-permute-start.3 = (f32[64,256]{1,0:T(8,128)S(1)}, f32[64,256]{1,0:T(8,128)S(1)}, u32[]{:S(2)}, u32[]{:S(2)}) collective-permute-start(f32[64,256]{1,0:T(8,128)S(1)} %add.13), channel_id=1, source_target_pairs={{0,2},{1,3},{2,0},{3,1},{4,6},{5,7},{6,4},{7,5},{8,10},{9,11},{10,... | collective-permute-start | bytes 196616 | tf_op jit(solution)/shard_map/ppermute | solution.py:148
  27.5 4.7 %collective-permute-start.8 = (f32[64,256]{1,0:T(8,128)S(1)}, f32[64,256]{1,0:T(8,128)S(1)}, u32[]{:S(2)}, u32[]{:S(2)}) collective-permute-start(f32[64,256]{1,0:T(8,128)S(1)} %add.15), channel_id=1, source_target_pairs={{0,2},{1,3},{2,0},{3,1},{4,6},{5,7},{6,4},{7,5},{8,10},{9,11},{10,... | collective-permute-start | bytes 196616 | tf_op jit(solution)/shard_map/ppermute | solution.py:148

commit v5 on v4

--- a/solution.py
+++ b/solution.py
@@ -8,7 +8,7 @@
 from jax.sharding import PartitionSpec as P
 
 CHUNK = 1024
-DEPTH = 6
+DEPTH = 20
 
 
 def split(value):

time: 33.1 us -> 32.8 us (level)
  no operation moved by 1% of the time
where the time goes in v5:
time: 32.8 us; the launch traced here: 32.7 us
  starting transfers between devices  11.7 us (36%)
  Pallas kernels  11.5 us (35%)
  waiting for transfers between devices  8.62 us (26%)
  other arithmetic  0.78 us (2%)
    pallas_call x1, Pallas kernels, matmul(): pl.pallas_call(functools.partial(matmul_kernel, spans, pick), out_shape=(...  11.5 us
    ppermute x4, starting transfers between devices, permute(): return lax.ppermute(value, ('row', 'col'), pairs)  5.49 us
    ppermute x4, waiting for transfers between devices, permute(): return lax.ppermute(value, ('row', 'col'), pairs)  4.44 us
    ppermute x2, waiting for transfers between devices, square(): other.append(lax.ppermute(part, 'col', [(c, c ^ 2) for c in range(n_col)]))  3.6 us
    ppermute x1, starting transfers between devices, square(): relay = lax.ppermute(relay, 'col', [(c, c ^ 2) for c in range(n_col)])  3.01 us
    ppermute x2, starting transfers between devices, square(): part = part + lax.ppermute(part, 'col', [(c, c ^ 1) for c in range(n_col)])  1.64 us
    ppermute x2, starting transfers between devices, square(): other.append(lax.ppermute(part, 'col', [(c, c ^ 2) for c in range(n_col)]))  1.59 us
    concatenate x1, other arithmetic, square(): return jnp.concatenate(top + bottom, 0)  0.72 us
  transfers between devices with their start and end apart: 9, of which 6 were waited for; matrix products, arithmetic and copies ran while one was open for 0% of the time, Pallas kernels for 0%

profile of v5, /device:TPU:0, one launch (start us, length us, event | category | flops | bytes accessed | tf_op | source)
XLA Modules:
  0.0 32.7 jit_solution(17513493349031989220)
XLA Ops:
  0.0 11.5 %shard_map.28 = (f32[64,256]{1,0:T(8,128)S(1)}, f32[64,256]{1,0:T(8,128)S(1)}, f32[64,256]{1,0:T(8,128)S(1)}, f32[64,256]{1,0:T(8,128)S(1)}) custom-call(f32[256,16384]{1,0:T(8,128)} %a_hbm.1, f32[16384,256]{1,0:T(8,128)} %b_hbm.1), custom_call_target="tpu_custom_call" | custom-call | tf_op jit(solution)/shard_map/pallas_call | solution.py:89
  11.5 3.0 %collective-permute-start.4 = (f32[64,256]{1,0:T(8,128)S(1)}, f32[64,256]{1,0:T(8,128)S(1)}, u32[]{:S(2)}, u32[]{:S(2)}) collective-permute-start(f32[64,256]{1,0:T(8,128)S(1)} %get-tuple-element.13), channel_id=1, source_target_pairs={{0,2},{1,3},{2,0},{3,1},{4,6},{5,7},{6,4},{7,5},{8,10},{9,11},{10,... | collective-permute-start | bytes 196616 | tf_op jit(solution)/shard_map/ppermute | solution.py:138
  14.6 0.0 collective-permute-start
  14.6 3.9 %collective-permute-start.1 = (f32[64,256]{1,0:T(8,128)S(1)}, f32[64,256]{1,0:T(8,128)S(1)}, u32[]{:S(2)}, u32[]{:S(2)}) collective-permute-start(f32[64,256]{1,0:T(8,128)S(1)} %get-tuple-element.12), channel_id=1, source_target_pairs={{0,3},{1,7},{2,11},{3,15},{4,2},{5,6},{6,10},{7,14},{8,1},{9,5},{1... | collective-permute-start | bytes 196616 | tf_op jit(solution)/shard_map/ppermute | solution.py:109
  18.5 0.0 collective-permute-done.4
  18.5 0.0 collective-permute-start.5
  18.5 1.6 %collective-permute-start.6 = (f32[64,256]{1,0:T(8,128)S(1)}, f32[64,256]{1,0:T(8,128)S(1)}, u32[]{:S(2)}, u32[]{:S(2)}) collective-permute-start(f32[64,256]{1,0:T(8,128)S(1)} %get-tuple-element.16), channel_id=1, source_target_pairs={{0,3},{1,7},{2,11},{3,15},{4,2},{5,6},{6,10},{7,14},{8,1},{9,5},{1... | collective-permute-start | bytes 196616 | tf_op jit(solution)/shard_map/ppermute | solution.py:109
  20.0 0.0 collective-permute-done
  20.0 2.3 %collective-permute-done.1 = f32[64,256]{1,0:T(8,128)S(1)} collective-permute-done((f32[64,256]{1,0:T(8,128)S(1)}, f32[64,256]{1,0:T(8,128)S(1)}, u32[]{:S(2)}, u32[]{:S(2)}) %collective-permute-start.1) | collective-permute-done | bytes 65568 | tf_op jit(solution)/shard_map/ppermute | solution.py:109
  22.4 1.4 %collective-permute-start.2 = (f32[64,256]{1,0:T(8,128)S(1)}, f32[64,256]{1,0:T(8,128)S(1)}, u32[]{:S(2)}, u32[]{:S(2)}) collective-permute-start(f32[64,256]{1,0:T(8,128)S(1)} %add.12), channel_id=1, source_target_pairs={{0,1},{1,0},{2,3},{3,2},{4,5},{5,4},{6,7},{7,6},{8,9},{9,8},{10,11... | collective-permute-start | bytes 196616 | tf_op jit(solution)/shard_map/ppermute | solution.py:146
  23.8 0.5 %collective-permute-done.5 = f32[64,256]{1,0:T(8,128)S(1)} collective-permute-done((f32[64,256]{1,0:T(8,128)S(1)}, f32[64,256]{1,0:T(8,128)S(1)}, u32[]{:S(2)}, u32[]{:S(2)}) %collective-permute-start.5) | collective-permute-done | bytes 65568 | tf_op jit(solution)/shard_map/ppermute | solution.py:109
  24.3 1.6 %collective-permute-done.6 = f32[64,256]{1,0:T(8,128)S(1)} collective-permute-done((f32[64,256]{1,0:T(8,128)S(1)}, f32[64,256]{1,0:T(8,128)S(1)}, u32[]{:S(2)}, u32[]{:S(2)}) %collective-permute-start.6) | collective-permute-done | bytes 65568 | tf_op jit(solution)/shard_map/ppermute | solution.py:109
  25.9 0.3 collective-permute-start.7
  26.1 0.0 collective-permute-done.2
  26.2 0.5 %collective-permute-start.3 = (f32[64,256]{1,0:T(8,128)S(1)}, f32[64,256]{1,0:T(8,128)S(1)}, u32[]{:S(2)}, u32[]{:S(2)}) collective-permute-start(f32[64,256]{1,0:T(8,128)S(1)} %add.13), channel_id=1, source_target_pairs={{0,2},{1,3},{2,0},{3,1},{4,6},{5,7},{6,4},{7,5},{8,10},{9,11},{10,... | collective-permute-start | bytes 196616 | tf_op jit(solution)/shard_map/ppermute | solution.py:148
  26.6 0.6 %collective-permute-done.7 = f32[64,256]{1,0:T(8,128)S(1)} collective-permute-done((f32[64,256]{1,0:T(8,128)S(1)}, f32[64,256]{1,0:T(8,128)S(1)}, u32[]{:S(2)}, u32[]{:S(2)}) %collective-permute-start.7) | collective-permute-done | bytes 65568 | tf_op jit(solution)/shard_map/ppermute | solution.py:146
  27.2 1.1 %collective-permute-start.8 = (f32[64,256]{1,0:T(8,128)S(1)}, f32[64,256]{1,0:T(8,128)S(1)}, u32[]{:S(2)}, u32[]{:S(2)}) collective-permute-start(f32[64,256]{1,0:T(8,128)S(1)} %add.15), channel_id=1, source_target_pairs={{0,2},{1,3},{2,0},{3,1},{4,6},{5,7},{6,4},{7,5},{8,10},{9,11},{10,... | collective-permute-start | bytes 196616 | tf_op jit(solution)/shard_map/ppermute | solution.py:148
  28.3 2.7 %collective-permute-done.3 = f32[64,256]{1,0:T(8,128)S(1)} collective-permute-done((f32[64,256]{1,0:T(8,128)S(1)}, f32[64,256]{1,0:T(8,128)S(1)}, u32[]{:S(2)}, u32[]{:S(2)}) %collective-permute-start.3) | collective-permute-done | bytes 65568 | tf_op jit(solution)/shard_map/ppermute | solution.py:148
  31.0 0.9 %collective-permute-done.8 = f32[64,256]{1,0:T(8,128)S(1)} collective-permute-done((f32[64,256]{1,0:T(8,128)S(1)}, f32[64,256]{1,0:T(8,128)S(1)}, u32[]{:S(2)}, u32[]{:S(2)}) %collective-permute-start.8) | collective-permute-done | bytes 65568 | tf_op jit(solution)/shard_map/ppermute | solution.py:148
  32.0 0.7 %pad_maximum_fusion = f32[256,256]{1,0:T(8,128)} fusion(f32[64,256]{1,0:T(8,128)S(1)} %get-tuple-element.20, f32[64,256]{1,0:T(8,128)S(1)} %get-tuple-element.18, f32[64,256]{1,0:T(8,128)S(1)} %get-tuple-element.19, f32[64,256]{1,0:T(8,128)S(1)} %get-tuple-element.17), kind=kLoop, calls=%fused_computation | loop fusion | flops 196608 | bytes 524288 | tf_op jit(solution)/shard_map/concatenate | solution.py:152
  (6 shorter events, 0.1 us)
Async XLA Ops:
  11.5 6.9 %collective-permute-start.4 = (f32[64,256]{1,0:T(8,128)S(1)}, f32[64,256]{1,0:T(8,128)S(1)}, u32[]{:S(2)}, u32[]{:S(2)}) collective-permute-start(f32[64,256]{1,0:T(8,128)S(1)} %get-tuple-element.13), channel_id=1, source_target_pairs={{0,2},{1,3},{2,0},{3,1},{4,6},{5,7},{6,4},{7,5},{8,10},{9,11},{10,... | collective-permute-start | bytes 196616 | tf_op jit(solution)/shard_map/ppermute | solution.py:138
  14.6 5.5 %collective-permute-start = (f32[64,256]{1,0:T(8,128)S(1)}, f32[64,256]{1,0:T(8,128)S(1)}, u32[]{:S(2)}, u32[]{:S(2)}) collective-permute-start(f32[64,256]{1,0:T(8,128)S(1)} %get-tuple-element.11), channel_id=1, source_target_pairs={{0,1},{1,5},{2,9},{3,13},{4,0},{5,4},{6,8},{7,12},{8,3},{9,7},{10,... | collective-permute-start | bytes 196616 | tf_op jit(solution)/shard_map/ppermute | solution.py:109
  14.6 7.8 %collective-permute-start.1 = (f32[64,256]{1,0:T(8,128)S(1)}, f32[64,256]{1,0:T(8,128)S(1)}, u32[]{:S(2)}, u32[]{:S(2)}) collective-permute-start(f32[64,256]{1,0:T(8,128)S(1)} %get-tuple-element.12), channel_id=1, source_target_pairs={{0,3},{1,7},{2,11},{3,15},{4,2},{5,6},{6,10},{7,14},{8,1},{9,5},{1... | collective-permute-start | bytes 196616 | tf_op jit(solution)/shard_map/ppermute | solution.py:109
  18.5 5.8 %collective-permute-start.5 = (f32[64,256]{1,0:T(8,128)S(1)}, f32[64,256]{1,0:T(8,128)S(1)}, u32[]{:S(2)}, u32[]{:S(2)}) collective-permute-start(f32[64,256]{1,0:T(8,128)S(1)} %collective-permute-done.4), channel_id=1, source_target_pairs={{0,9},{1,13},{2,1},{3,5},{4,8},{5,12},{6,0},{7,4},{8,11},{9,15},{1... | collective-permute-start | bytes 196616 | tf_op jit(solution)/shard_map/ppermute | solution.py:109
  18.5 7.4 %collective-permute-start.6 = (f32[64,256]{1,0:T(8,128)S(1)}, f32[64,256]{1,0:T(8,128)S(1)}, u32[]{:S(2)}, u32[]{:S(2)}) collective-permute-start(f32[64,256]{1,0:T(8,128)S(1)} %get-tuple-element.16), channel_id=1, source_target_pairs={{0,3},{1,7},{2,11},{3,15},{4,2},{5,6},{6,10},{7,14},{8,1},{9,5},{1... | collective-permute-start | bytes 196616 | tf_op jit(solution)/shard_map/ppermute | solution.py:109
  22.4 3.8 %collective-permute-start.2 = (f32[64,256]{1,0:T(8,128)S(1)}, f32[64,256]{1,0:T(8,128)S(1)}, u32[]{:S(2)}, u32[]{:S(2)}) collective-permute-start(f32[64,256]{1,0:T(8,128)S(1)} %add.12), channel_id=1, source_target_pairs={{0,1},{1,0},{2,3},{3,2},{4,5},{5,4},{6,7},{7,6},{8,9},{9,8},{10,11... | collective-permute-start | bytes 196616 | tf_op jit(solution)/shard_map/ppermute | solution.py:146
  25.9 1.3 %collective-permute-start.7 = (f32[64,256]{1,0:T(8,128)S(1)}, f32[64,256]{1,0:T(8,128)S(1)}, u32[]{:S(2)}, u32[]{:S(2)}) collective-permute-start(f32[64,256]{1,0:T(8,128)S(1)} %add.14), channel_id=1, source_target_pairs={{0,1},{1,0},{2,3},{3,2},{4,5},{5,4},{6,7},{7,6},{8,9},{9,8},{10,11... | collective-permute-start | bytes 196616 | tf_op jit(solution)/shard_map/ppermute | solution.py:146
  26.2 4.9 %collective-permute-start.3 = (f32[64,256]{1,0:T(8,128)S(1)}, f32[64,256]{1,0:T(8,128)S(1)}, u32[]{:S(2)}, u32[]{:S(2)}) collective-permute-start(f32[64,256]{1,0:T(8,128)S(1)} %add.13), channel_id=1, source_target_pairs={{0,2},{1,3},{2,0},{3,1},{4,6},{5,7},{6,4},{7,5},{8,10},{9,11},{10,... | collective-permute-start | bytes 196616 | tf_op jit(solution)/shard_map/ppermute | solution.py:148
  27.2 4.7 %collective-permute-start.8 = (f32[64,256]{1,0:T(8,128)S(1)}, f32[64,256]{1,0:T(8,128)S(1)}, u32[]{:S(2)}, u32[]{:S(2)}) collective-permute-start(f32[64,256]{1,0:T(8,128)S(1)} %add.15), channel_id=1, source_target_pairs={{0,2},{1,3},{2,0},{3,1},{4,6},{5,7},{6,4},{7,5},{8,10},{9,11},{10,... | collective-permute-start | bytes 196616 | tf_op jit(solution)/shard_map/ppermute | solution.py:148

commit v6 on v5

--- a/solution.py
+++ b/solution.py
@@ -27,7 +27,7 @@
     while left > CHUNK:
         sizes.append(CHUNK)
         left -= CHUNK
-    while left > 256 and left % 256 == 0:
+    while left > 128 and left % 256 == 0:
         sizes.append(left // 2)
         left -= left // 2
     sizes.append(left)

time: 32.8 us -> 33 us (level)
  no operation moved by 1% of the time
where the time goes in v6:
time: 33 us; the launch traced here: 32.8 us
  Pallas kernels  11.7 us (35%)
  starting transfers between devices  11.7 us (35%)
  waiting for transfers between devices  8.62 us (26%)
  other arithmetic  0.78 us (2%)
    pallas_call x1, Pallas kernels, matmul(): pl.pallas_call(functools.partial(matmul_kernel, spans, pick), out_shape=(...  11.7 us
    ppermute x4, starting transfers between devices, permute(): return lax.ppermute(value, ('row', 'col'), pairs)  5.49 us
    ppermute x4, waiting for transfers between devices, permute(): return lax.ppermute(value, ('row', 'col'), pairs)  4.44 us
    ppermute x2, waiting for transfers between devices, square(): other.append(lax.ppermute(part, 'col', [(c, c ^ 2) for c in range(n_col)]))  3.6 us
    ppermute x1, starting transfers between devices, square(): relay = lax.ppermute(relay, 'col', [(c, c ^ 2) for c in range(n_col)])  3.01 us
    ppermute x2, starting transfers between devices, square(): part = part + lax.ppermute(part, 'col', [(c, c ^ 1) for c in range(n_col)])  1.64 us
    ppermute x2, starting transfers between devices, square(): other.append(lax.ppermute(part, 'col', [(c, c ^ 2) for c in range(n_col)]))  1.59 us
    concatenate x1, other arithmetic, square(): return jnp.concatenate(top + bottom, 0)  0.72 us
  transfers between devices with their start and end apart: 9, of which 6 were waited for; matrix products, arithmetic and copies ran while one was open for 0% of the time, Pallas kernels for 0%

profile of v6, /device:TPU:0, one launch (start us, length us, event | category | flops | bytes accessed | tf_op | source)
XLA Modules:
  0.0 32.8 jit_solution(6296101282269730062)
XLA Ops:
  0.0 11.7 %shard_map.28 = (f32[64,256]{1,0:T(8,128)S(1)}, f32[64,256]{1,0:T(8,128)S(1)}, f32[64,256]{1,0:T(8,128)S(1)}, f32[64,256]{1,0:T(8,128)S(1)}) custom-call(f32[256,16384]{1,0:T(8,128)} %a_hbm.1, f32[16384,256]{1,0:T(8,128)} %b_hbm.1), custom_call_target="tpu_custom_call" | custom-call | tf_op jit(solution)/shard_map/pallas_call | solution.py:89
  11.7 3.0 %collective-permute-start.4 = (f32[64,256]{1,0:T(8,128)S(1)}, f32[64,256]{1,0:T(8,128)S(1)}, u32[]{:S(2)}, u32[]{:S(2)}) collective-permute-start(f32[64,256]{1,0:T(8,128)S(1)} %get-tuple-element.13), channel_id=1, source_target_pairs={{0,2},{1,3},{2,0},{3,1},{4,6},{5,7},{6,4},{7,5},{8,10},{9,11},{10,... | collective-permute-start | bytes 196616 | tf_op jit(solution)/shard_map/ppermute | solution.py:138
  14.7 0.0 collective-permute-start
  14.7 3.9 %collective-permute-start.1 = (f32[64,256]{1,0:T(8,128)S(1)}, f32[64,256]{1,0:T(8,128)S(1)}, u32[]{:S(2)}, u32[]{:S(2)}) collective-permute-start(f32[64,256]{1,0:T(8,128)S(1)} %get-tuple-element.12), channel_id=1, source_target_pairs={{0,3},{1,7},{2,11},{3,15},{4,2},{5,6},{6,10},{7,14},{8,1},{9,5},{1... | collective-permute-start | bytes 196616 | tf_op jit(solution)/shard_map/ppermute | solution.py:109
  18.6 0.0 collective-permute-done.4
  18.6 0.0 collective-permute-start.5
  18.6 1.6 %collective-permute-start.6 = (f32[64,256]{1,0:T(8,128)S(1)}, f32[64,256]{1,0:T(8,128)S(1)}, u32[]{:S(2)}, u32[]{:S(2)}) collective-permute-start(f32[64,256]{1,0:T(8,128)S(1)} %get-tuple-element.16), channel_id=1, source_target_pairs={{0,3},{1,7},{2,11},{3,15},{4,2},{5,6},{6,10},{7,14},{8,1},{9,5},{1... | collective-permute-start | bytes 196616 | tf_op jit(solution)/shard_map/ppermute | solution.py:109
  20.2 0.0 collective-permute-done
  20.2 2.3 %collective-permute-done.1 = f32[64,256]{1,0:T(8,128)S(1)} collective-permute-done((f32[64,256]{1,0:T(8,128)S(1)}, f32[64,256]{1,0:T(8,128)S(1)}, u32[]{:S(2)}, u32[]{:S(2)}) %collective-permute-start.1) | collective-permute-done | bytes 65568 | tf_op jit(solution)/shard_map/ppermute | solution.py:109
  22.5 1.4 %collective-permute-start.2 = (f32[64,256]{1,0:T(8,128)S(1)}, f32[64,256]{1,0:T(8,128)S(1)}, u32[]{:S(2)}, u32[]{:S(2)}) collective-permute-start(f32[64,256]{1,0:T(8,128)S(1)} %add.12), channel_id=1, source_target_pairs={{0,1},{1,0},{2,3},{3,2},{4,5},{5,4},{6,7},{7,6},{8,9},{9,8},{10,11... | collective-permute-start | bytes 196616 | tf_op jit(solution)/shard_map/ppermute | solution.py:146
  23.9 0.5 %collective-permute-done.5 = f32[64,256]{1,0:T(8,128)S(1)} collective-permute-done((f32[64,256]{1,0:T(8,128)S(1)}, f32[64,256]{1,0:T(8,128)S(1)}, u32[]{:S(2)}, u32[]{:S(2)}) %collective-permute-start.5) | collective-permute-done | bytes 65568 | tf_op jit(solution)/shard_map/ppermute | solution.py:109
  24.4 1.6 %collective-permute-done.6 = f32[64,256]{1,0:T(8,128)S(1)} collective-permute-done((f32[64,256]{1,0:T(8,128)S(1)}, f32[64,256]{1,0:T(8,128)S(1)}, u32[]{:S(2)}, u32[]{:S(2)}) %collective-permute-start.6) | collective-permute-done | bytes 65568 | tf_op jit(solution)/shard_map/ppermute | solution.py:109
  26.0 0.3 collective-permute-start.7
  26.3 0.0 collective-permute-done.2
  26.3 0.5 %collective-permute-start.3 = (f32[64,256]{1,0:T(8,128)S(1)}, f32[64,256]{1,0:T(8,128)S(1)}, u32[]{:S(2)}, u32[]{:S(2)}) collective-permute-start(f32[64,256]{1,0:T(8,128)S(1)} %add.13), channel_id=1, source_target_pairs={{0,2},{1,3},{2,0},{3,1},{4,6},{5,7},{6,4},{7,5},{8,10},{9,11},{10,... | collective-permute-start | bytes 196616 | tf_op jit(solution)/shard_map/ppermute | solution.py:148
  26.8 0.6 %collective-permute-done.7 = f32[64,256]{1,0:T(8,128)S(1)} collective-permute-done((f32[64,256]{1,0:T(8,128)S(1)}, f32[64,256]{1,0:T(8,128)S(1)}, u32[]{:S(2)}, u32[]{:S(2)}) %collective-permute-start.7) | collective-permute-done | bytes 65568 | tf_op jit(solution)/shard_map/ppermute | solution.py:146
  27.4 1.1 %collective-permute-start.8 = (f32[64,256]{1,0:T(8,128)S(1)}, f32[64,256]{1,0:T(8,128)S(1)}, u32[]{:S(2)}, u32[]{:S(2)}) collective-permute-start(f32[64,256]{1,0:T(8,128)S(1)} %add.15), channel_id=1, source_target_pairs={{0,2},{1,3},{2,0},{3,1},{4,6},{5,7},{6,4},{7,5},{8,10},{9,11},{10,... | collective-permute-start | bytes 196616 | tf_op jit(solution)/shard_map/ppermute | solution.py:148
  28.5 2.7 %collective-permute-done.3 = f32[64,256]{1,0:T(8,128)S(1)} collective-permute-done((f32[64,256]{1,0:T(8,128)S(1)}, f32[64,256]{1,0:T(8,128)S(1)}, u32[]{:S(2)}, u32[]{:S(2)}) %collective-permute-start.3) | collective-permute-done | bytes 65568 | tf_op jit(solution)/shard_map/ppermute | solution.py:148
  31.2 0.9 %collective-permute-done.8 = f32[64,256]{1,0:T(8,128)S(1)} collective-permute-done((f32[64,256]{1,0:T(8,128)S(1)}, f32[64,256]{1,0:T(8,128)S(1)}, u32[]{:S(2)}, u32[]{:S(2)}) %collective-permute-start.8) | collective-permute-done | bytes 65568 | tf_op jit(solution)/shard_map/ppermute | solution.py:148
  32.1 0.7 %pad_maximum_fusion = f32[256,256]{1,0:T(8,128)} fusion(f32[64,256]{1,0:T(8,128)S(1)} %get-tuple-element.20, f32[64,256]{1,0:T(8,128)S(1)} %get-tuple-element.18, f32[64,256]{1,0:T(8,128)S(1)} %get-tuple-element.19, f32[64,256]{1,0:T(8,128)S(1)} %get-tuple-element.17), kind=kLoop, calls=%fused_computation | loop fusion | flops 196608 | bytes 524288 | tf_op jit(solution)/shard_map/concatenate | solution.py:152
  (6 shorter events, 0.1 us)
Async XLA Ops:
  11.7 6.9 %collective-permute-start.4 = (f32[64,256]{1,0:T(8,128)S(1)}, f32[64,256]{1,0:T(8,128)S(1)}, u32[]{:S(2)}, u32[]{:S(2)}) collective-permute-start(f32[64,256]{1,0:T(8,128)S(1)} %get-tuple-element.13), channel_id=1, source_target_pairs={{0,2},{1,3},{2,0},{3,1},{4,6},{5,7},{6,4},{7,5},{8,10},{9,11},{10,... | collective-permute-start | bytes 196616 | tf_op jit(solution)/shard_map/ppermute | solution.py:138
  14.7 5.5 %collective-permute-start = (f32[64,256]{1,0:T(8,128)S(1)}, f32[64,256]{1,0:T(8,128)S(1)}, u32[]{:S(2)}, u32[]{:S(2)}) collective-permute-start(f32[64,256]{1,0:T(8,128)S(1)} %get-tuple-element.11), channel_id=1, source_target_pairs={{0,1},{1,5},{2,9},{3,13},{4,0},{5,4},{6,8},{7,12},{8,3},{9,7},{10,... | collective-permute-start | bytes 196616 | tf_op jit(solution)/shard_map/ppermute | solution.py:109
  14.7 7.8 %collective-permute-start.1 = (f32[64,256]{1,0:T(8,128)S(1)}, f32[64,256]{1,0:T(8,128)S(1)}, u32[]{:S(2)}, u32[]{:S(2)}) collective-permute-start(f32[64,256]{1,0:T(8,128)S(1)} %get-tuple-element.12), channel_id=1, source_target_pairs={{0,3},{1,7},{2,11},{3,15},{4,2},{5,6},{6,10},{7,14},{8,1},{9,5},{1... | collective-permute-start | bytes 196616 | tf_op jit(solution)/shard_map/ppermute | solution.py:109
  18.6 5.8 %collective-permute-start.5 = (f32[64,256]{1,0:T(8,128)S(1)}, f32[64,256]{1,0:T(8,128)S(1)}, u32[]{:S(2)}, u32[]{:S(2)}) collective-permute-start(f32[64,256]{1,0:T(8,128)S(1)} %collective-permute-done.4), channel_id=1, source_target_pairs={{0,9},{1,13},{2,1},{3,5},{4,8},{5,12},{6,0},{7,4},{8,11},{9,15},{1... | collective-permute-start | bytes 196616 | tf_op jit(solution)/shard_map/ppermute | solution.py:109
  18.6 7.4 %collective-permute-start.6 = (f32[64,256]{1,0:T(8,128)S(1)}, f32[64,256]{1,0:T(8,128)S(1)}, u32[]{:S(2)}, u32[]{:S(2)}) collective-permute-start(f32[64,256]{1,0:T(8,128)S(1)} %get-tuple-element.16), channel_id=1, source_target_pairs={{0,3},{1,7},{2,11},{3,15},{4,2},{5,6},{6,10},{7,14},{8,1},{9,5},{1... | collective-permute-start | bytes 196616 | tf_op jit(solution)/shard_map/ppermute | solution.py:109
  22.5 3.8 %collective-permute-start.2 = (f32[64,256]{1,0:T(8,128)S(1)}, f32[64,256]{1,0:T(8,128)S(1)}, u32[]{:S(2)}, u32[]{:S(2)}) collective-permute-start(f32[64,256]{1,0:T(8,128)S(1)} %add.12), channel_id=1, source_target_pairs={{0,1},{1,0},{2,3},{3,2},{4,5},{5,4},{6,7},{7,6},{8,9},{9,8},{10,11... | collective-permute-start | bytes 196616 | tf_op jit(solution)/shard_map/ppermute | solution.py:146
  26.0 1.3 %collective-permute-start.7 = (f32[64,256]{1,0:T(8,128)S(1)}, f32[64,256]{1,0:T(8,128)S(1)}, u32[]{:S(2)}, u32[]{:S(2)}) collective-permute-start(f32[64,256]{1,0:T(8,128)S(1)} %add.14), channel_id=1, source_target_pairs={{0,1},{1,0},{2,3},{3,2},{4,5},{5,4},{6,7},{7,6},{8,9},{9,8},{10,11... | collective-permute-start | bytes 196616 | tf_op jit(solution)/shard_map/ppermute | solution.py:146
  26.3 4.9 %collective-permute-start.3 = (f32[64,256]{1,0:T(8,128)S(1)}, f32[64,256]{1,0:T(8,128)S(1)}, u32[]{:S(2)}, u32[]{:S(2)}) collective-permute-start(f32[64,256]{1,0:T(8,128)S(1)} %add.13), channel_id=1, source_target_pairs={{0,2},{1,3},{2,0},{3,1},{4,6},{5,7},{6,4},{7,5},{8,10},{9,11},{10,... | collective-permute-start | bytes 196616 | tf_op jit(solution)/shard_map/ppermute | solution.py:148
  27.4 4.7 %collective-permute-start.8 = (f32[64,256]{1,0:T(8,128)S(1)}, f32[64,256]{1,0:T(8,128)S(1)}, u32[]{:S(2)}, u32[]{:S(2)}) collective-permute-start(f32[64,256]{1,0:T(8,128)S(1)} %add.15), channel_id=1, source_target_pairs={{0,2},{1,3},{2,0},{3,1},{4,6},{5,7},{6,4},{7,5},{8,10},{9,11},{10,... | collective-permute-start | bytes 196616 | tf_op jit(solution)/shard_map/ppermute | solution.py:148
